TPU v7x, 32 devices: a whole 2x2x4 slice. The times are simulated.
32 devices in a mesh: seq: 8 (over z, y), head: 4 (over x, core).
Axes of the slice: x: 2, y: 2, z: 4, core: 2. Of those that a mesh axis runs over, the one named last changes fastest.
Arguments:
- queries: bfloat16 [8, 1024, 128], P('head', 'seq')
- keys: bfloat16 [8, 1024, 128], P('head', 'seq')
- values: bfloat16 [8, 1024, 128], P('head', 'seq'), may hold values from -6 to 6
- grad_out: bfloat16 [8, 1024, 128], P('head', 'seq'), may hold values from -96 to 96
- rand_ids: int32 [8, 16, 3], P('head', 'seq'), may hold values from 0 to 15, as said below
- global_ids: int32 [2], replicated, may hold values from 0 to 15
Outputs:
- grad_queries: bfloat16 [8, 1024, 128], P('head', 'seq')
- grad_keys: bfloat16 [8, 1024, 128], P('head', 'seq')
- grad_values: bfloat16 [8, 1024, 128], P('head', 'seq')
Inputs may be any that keep to these rules, and one draw needn't show every extreme that they name: `rand_ids`: for each head and slot j there is one number M, 0 <= M < 8, such that every query block b names in slot j a block e * 2 + l with e = (b // 2) XOR M and 0 <= l < 2.
All inputs are finite; a program needn't handle non-finite values.
Results may differ from a plain program's by a relative error of at most 0.03.
Values may be sent and summed in bfloat16 or wider, within the bound.
No kernel may reach another device: no remote copies, remote signals or barrier semaphores. Data moves between devices by JAX's collectives and lax.ppermute only.
A program may use at most 64 MiB of HBM per device.

v0:
```python
import math

import jax
import jax.numpy as jnp
from jax import lax
from jax.sharding import PartitionSpec as P


def with_halo(value, sides, width):
    for axis, dim in sides:
        peers, length = (lax.axis_size(axis), value.shape[dim])
        up = [(i, (i + 1) % peers) for i in range(peers - 1)]
        down = [(j, i) for i, j in up]
        last = lax.slice_in_dim(value, length - width, length, axis=dim)
        initial = lax.slice_in_dim(value, 0, width, axis=dim)
        before = lax.ppermute(last, axis, up)
        after = lax.ppermute(initial, axis, down)
        value = jnp.concatenate([before, value, after], axis=dim)
    return value


def swapped(value, axis, distance):
    mask = 2**distance
    pairs = [(source, source ^ mask) for source in range(lax.axis_size(axis))]
    return lax.ppermute(value, axis, pairs)


def section_list(section_count):
    return list(range(section_count))


def on_device(queries, keys, values, grad_out, rand_ids, global_ids):
    head_count, row_count, head_width = queries.shape
    block_count = rand_ids.shape[1]
    slot_count = rand_ids.shape[2]
    block_rows = row_count // block_count
    global_count = global_ids.shape[0]
    slot_total = 3 + global_count + slot_count
    device = lax.axis_index("seq")
    seq_count = lax.axis_size("seq")
    sections = section_list(seq_count.bit_length() - 1)
    score_scale = 1.0 / math.sqrt(head_width)
    key_vals = jnp.stack([keys, values])
    padded = with_halo(key_vals, (("seq", 2),), block_rows)
    padded_blocks = padded.reshape(2, head_count, block_count + 2, block_rows, head_width)
    window = jnp.stack(
        [
            padded_blocks[:, :, 0:block_count],
            padded_blocks[:, :, 1 : block_count + 1],
            padded_blocks[:, :, 2 : block_count + 2],
        ],
        3,
    )
    key_blocks = key_vals.reshape(2, head_count, block_count, block_rows, head_width)
    global_local = global_ids % block_count
    global_owner = global_ids // block_count
    owned = (global_owner == device).astype(jnp.float32)
    picked = jnp.take(key_blocks, global_local, axis=2).astype(jnp.float32)
    global_sum = lax.psum(picked * owned[None, None, :, None, None], "seq")
    global_kv = global_sum.astype(jnp.bfloat16)
    global_keys = jnp.broadcast_to(
        global_kv[:, :, None], (2, head_count, block_count, global_count, block_rows, head_width)
    )
    xor_masks = jnp.bitwise_xor(rand_ids[:, 0, :] // block_count, device)
    pieces = []
    for slot_index in range(slot_count):
        moving = key_vals
        for bit_index in sections:
            arrived = swapped(moving, "seq", bit_index)
            flag_now = jnp.right_shift(xor_masks[:, slot_index], bit_index) & 1 == 1
            moving = jnp.where(flag_now[None, :, None, None], arrived, moving)
        pieces.append(moving)
    routed = jnp.stack(pieces)
    routed_blocks = routed.reshape(slot_count, 2, head_count, block_count, block_rows, head_width)
    random_local = rand_ids % block_count
    local_onehot = (random_local[..., None] == jnp.arange(block_count, dtype=jnp.int32)).astype(
        jnp.bfloat16
    )
    random_keys = jnp.einsum(
        "hqjl,jchlbd->chqjbd", local_onehot, routed_blocks, preferred_element_type=jnp.float32
    ).astype(jnp.bfloat16)
    all_keys = jnp.concatenate([window, global_keys, random_keys], axis=3)
    key_list = all_keys[0].reshape(head_count, block_count, slot_total * block_rows, head_width)
    value_list = all_keys[1].reshape(head_count, block_count, slot_total * block_rows, head_width)
    block_range = jnp.arange(block_count, dtype=jnp.int32)
    left_valid = jnp.logical_not((block_range == 0) & (device == 0))
    right_valid = jnp.logical_not((block_range == block_count - 1) & (device == seq_count - 1))
    valid = jnp.concatenate(
        [
            left_valid[:, None],
            jnp.ones((block_count, 1), bool),
            right_valid[:, None],
            jnp.ones((block_count, global_count + slot_count), bool),
        ],
        1,
    )
    mask = jnp.repeat(valid, block_rows, axis=1)[None, :, None, :]
    query_blocks = queries.reshape(head_count, block_count, block_rows, head_width)
    grad_blocks = grad_out.reshape(head_count, block_count, block_rows, head_width)
    scores = (
        jnp.einsum("hnqd,hnkd->hnqk", query_blocks, key_list, preferred_element_type=jnp.float32)
        * score_scale
    )
    row_max = jnp.max(jnp.where(mask, scores, -1e30), -1)
    total = jnp.sum(jnp.where(mask, jnp.exp(scores - row_max[..., None]), 0.0), -1)
    log_total = row_max + jnp.log(total)
    probs = jnp.where(mask, jnp.exp(scores - log_total[..., None]), 0.0)
    probs_low = probs.astype(jnp.bfloat16)
    output = jnp.einsum(
        "hnqk,hnkd->hnqd", probs_low, value_list, preferred_element_type=jnp.float32
    )
    row_dot = jnp.sum(grad_blocks.astype(jnp.float32) * output, -1)
    grad_probs = jnp.einsum(
        "hnqd,hnkd->hnqk", grad_blocks, value_list, preferred_element_type=jnp.float32
    )
    scores_low = (probs * (grad_probs - row_dot[..., None])).astype(jnp.bfloat16)
    grad_query = score_scale * jnp.einsum(
        "hnqk,hnkd->hnqd", scores_low, key_list, preferred_element_type=jnp.float32
    )
    key_terms = score_scale * jnp.einsum(
        "hnqk,hnqd->hnkd", scores_low, query_blocks, preferred_element_type=jnp.float32
    )
    value_terms = jnp.einsum(
        "hnqk,hnqd->hnkd", probs_low, grad_blocks, preferred_element_type=jnp.float32
    )
    grads = jnp.stack([key_terms, value_terms]).reshape(
        2, head_count, block_count, slot_total, block_rows, head_width
    )
    no_pad = (0, 0)
    frame_sum = jnp.pad(grads[:, :, :, 0], (no_pad, no_pad, (0, 2), no_pad, no_pad))
    frame_sum = frame_sum + jnp.pad(grads[:, :, :, 1], (no_pad, no_pad, (1, 1), no_pad, no_pad))
    frame_sum = frame_sum + jnp.pad(grads[:, :, :, 2], (no_pad, no_pad, (2, 0), no_pad, no_pad))
    own_grads = frame_sum[:, :, 1 : block_count + 1]
    rim_parts = jnp.concatenate([frame_sum[:, :, 0], frame_sum[:, :, block_count + 1]], axis=2)
    rim_back = with_halo(rim_parts.astype(jnp.bfloat16), (("seq", 2),), block_rows).astype(
        rim_parts.dtype
    )
    own_grads = own_grads.at[:, :, 0].add(rim_back[:, :, 0:block_rows])
    own_grads = own_grads.at[:, :, block_count - 1].add(
        rim_back[:, :, 3 * block_rows : 4 * block_rows]
    )
    global_part = jnp.sum(grads[:, :, :, 3 : 3 + global_count], axis=2)
    global_total = lax.psum(global_part, "seq")
    global_onehot = (
        (global_local[:, None] == block_range[None, :]) & (global_owner == device)[:, None]
    ).astype(jnp.float32)
    own_grads = own_grads + jnp.einsum(
        "gn,chgbd->chnbd", global_onehot, global_total, precision=lax.Precision.HIGHEST
    )
    random_part = grads[:, :, :, 3 + global_count :]
    local_float = (random_local[..., None] == block_range).astype(jnp.float32)
    send_back = jnp.einsum(
        "hqjl,chqjbd->jchlbd", local_float, random_part, precision=lax.Precision.HIGHEST
    )
    send_back = send_back.astype(jnp.bfloat16).reshape(
        slot_count, 2, head_count, row_count, head_width
    )
    pieces = []
    for slot_index in range(slot_count):
        moving = send_back[slot_index]
        for bit_index in sections:
            arrived = swapped(moving, "seq", bit_index)
            flag_now = jnp.right_shift(xor_masks[:, slot_index], bit_index) & 1 == 1
            moving = jnp.where(flag_now[None, :, None, None], arrived, moving)
        pieces.append(moving)
    returned = jnp.stack(pieces)
    returned_sum = jnp.sum(returned.astype(jnp.float32), axis=0).reshape(
        2, head_count, block_count, block_rows, head_width
    )
    own_grads = own_grads + returned_sum
    grad_queries = grad_query.reshape(head_count, row_count, head_width).astype(jnp.bfloat16)
    grad_keys = own_grads[0].reshape(head_count, row_count, head_width).astype(jnp.bfloat16)
    grad_values = own_grads[1].reshape(head_count, row_count, head_width).astype(jnp.bfloat16)
    return (grad_queries, grad_keys, grad_values)


def solution(mesh):
    in_specs = (
        P("head", "seq", None),
        P("head", "seq", None),
        P("head", "seq", None),
        P("head", "seq", None),
        P("head", "seq", None),
        P(),
    )
    out_specs = (P("head", "seq", None), P("head", "seq", None), P("head", "seq", None))
    return jax.shard_map(
        on_device, mesh=mesh, in_specs=in_specs, out_specs=out_specs, check_vma=False
    )
```

profile of v0, /device:TPU:0, one launch (start us, length us, event | category | flops | bytes accessed | tf_op | source)
XLA Modules:
  0.0 174.2 jit_solution(11851105725441294419)
XLA Ops:
  7.2 0.9 fusion.24
  8.1 1.3 collective-permute-start.1
  9.4 5.5 %collective-permute-start = (bf16[2,2,64,128]{3,2,1,0:T(8,128)(2,1)S(1)}, bf16[2,2,64,128]{3,2,1,0:T(8,128)(2,1)S(1)}, u32[]{:S(2)}, u32[]{:S(2)}) collective-permute-start(bf16[2,2,64,128]{3,2,1,0:T(8,128)(2,1)S(1)} %get-tuple-element.60), channel_id=1, source_target_pairs={{0,4},{4,8},{8,12},{12,16},{16,20},{20,24},{24,28},{1,5},{5,9},{9,... | collective-permute-start | bytes 196616 | tf_op jit(solution)/shard_map/ppermute | solution.py:16
  15.0 3.0 %collective-permute-start.2 = (bf16[2,2,128,128]{3,2,1,0:T(8,128)(2,1)S(1)}, bf16[2,2,128,128]{3,2,1,0:T(8,128)(2,1)S(1)}, u32[]{:S(2)}, u32[]{:S(2)}) collective-permute-start(bf16[2,2,128,128]{3,2,1,0:T(8,128)(2,1)S(1)} %pad_maximum_fusion.7), channel_id=1, source_target_pairs={{0,4},{4,0},{8,12},{12,8},{16,20},{20,16},{24,28},{28,24},{1,5},{5... | collective-permute-start | bytes 393224 | tf_op jit(solution)/shard_map/ppermute | solution.py:25
  19.4 38.6 %all-reduce.7 = bf16[2,2,2,64,128]{4,3,1,0,2:T(8,128)(2,1)S(1)} all-reduce(f32[2,2,2,64,128]{4,3,1,0,2:T(8,128)S(1)} %multiply_bitcast_fusion), channel_id=1, replica_groups=mesh['seq'=8,'head'=4] {'seq'}, use_global_device_ids=true, to_apply=%region_0.1 | all-reduce | flops 65536 | bytes 393216 | tf_op jit(solution)/shard_map/psum | solution.py:59
  60.4 2.1 %collective-permute-start.5 = (bf16[2,2,128,128]{3,2,1,0:T(8,128)(2,1)S(1)}, bf16[2,2,128,128]{3,2,1,0:T(8,128)(2,1)S(1)}, u32[]{:S(2)}, u32[]{:S(2)}) collective-permute-start(bf16[2,2,128,128]{3,2,1,0:T(8,128)(2,1)S(1)} %get-tuple-element.54), channel_id=1, source_target_pairs={{0,8},{4,12},{8,0},{12,4},{16,24},{20,28},{24,16},{28,20},{1,9},{5... | collective-permute-start | bytes 393224 | tf_op jit(solution)/shard_map/ppermute | solution.py:25
  62.6 4.0 %collective-permute-done.7 = bf16[2,2,128,128]{3,2,1,0:T(8,128)(2,1)S(1)} collective-permute-done((bf16[2,2,128,128]{3,2,1,0:T(8,128)(2,1)S(1)}, bf16[2,2,128,128]{3,2,1,0:T(8,128)(2,1)S(1)}, u32[]{:S(2)}, u32[]{:S(2)}) %collective-permute-start.7) | collective-permute-done | bytes 131104 | tf_op jit(solution)/shard_map/ppermute | solution.py:25
  66.8 2.9 %collective-permute-done.5 = bf16[2,2,128,128]{3,2,1,0:T(8,128)(2,1)S(1)} collective-permute-done((bf16[2,2,128,128]{3,2,1,0:T(8,128)(2,1)S(1)}, bf16[2,2,128,128]{3,2,1,0:T(8,128)(2,1)S(1)}, u32[]{:S(2)}, u32[]{:S(2)}) %collective-permute-start.5) | collective-permute-done | bytes 131104 | tf_op jit(solution)/shard_map/ppermute | solution.py:25
  69.8 1.2 collective-permute-done.3
  71.2 1.7 %collective-permute-start.4 = (bf16[2,2,128,128]{3,2,1,0:T(8,128)(2,1)S(1)}, bf16[2,2,128,128]{3,2,1,0:T(8,128)(2,1)S(1)}, u32[]{:S(2)}, u32[]{:S(2)}) collective-permute-start(bf16[2,2,128,128]{3,2,1,0:T(8,128)(2,1)S(1)} %broadcast_select_fusion.13), channel_id=1, source_target_pairs={{0,16},{4,20},{8,24},{12,28},{16,0},{20,4},{24,8},{28,12},{1,17},{... | collective-permute-start | bytes 393224 | tf_op jit(solution)/shard_map/ppermute | solution.py:25
  72.9 3.4 %collective-permute-done.8 = bf16[2,2,128,128]{3,2,1,0:T(8,128)(2,1)S(1)} collective-permute-done((bf16[2,2,128,128]{3,2,1,0:T(8,128)(2,1)S(1)}, bf16[2,2,128,128]{3,2,1,0:T(8,128)(2,1)S(1)}, u32[]{:S(2)}, u32[]{:S(2)}) %collective-permute-start.8) | collective-permute-done | bytes 131104 | tf_op jit(solution)/shard_map/ppermute | solution.py:25
  76.5 1.7 collective-permute-done.6
  78.4 1.4 collective-permute-done.4
  80.8 1.2 fusion.49
  84.5 0.9 fusion.8
  86.1 1.3 collective-permute-start.10
  87.4 4.7 %collective-permute-start.9 = (bf16[2,2,64,128]{3,2,1,0:T(8,128)(2,1)S(1)}, bf16[2,2,64,128]{3,2,1,0:T(8,128)(2,1)S(1)}, u32[]{:S(2)}, u32[]{:S(2)}) collective-permute-start(bf16[2,2,64,128]{3,2,1,0:T(8,128)(2,1)S(1)} %get-tuple-element.50), channel_id=1, source_target_pairs={{0,4},{4,8},{8,12},{12,16},{16,20},{20,24},{24,28},{1,5},{5,9},{9,... | collective-permute-start | bytes 196616 | tf_op jit(solution)/shard_map/ppermute | solution.py:16
  92.2 0.9 copy.63
  93.1 1.9 %fusion.2 = bf16[3,2,2,2,64,128]{5,3,4,1,2,0:T(2,128)(2,1)S(1)} fusion(f32[2,2,2,3,64,128]{5,4,3,2,1,0:T(8,128)S(1)} %pad_maximum_fusion, s32[2,2,3]{1,0,2:T(2,128)S(1)} %copy.53), kind=kOutput, calls=%fused_computation.8 | convolution fusion | flops 4915224 | bytes 1179696 | tf_op jit(solution)/shard_map/hqjl,chqjbd->jchlbd/dot_general | solution.py:152
  95.5 2.1 %collective-permute-start.14 = (bf16[2,2,128,128]{3,2,1,0:T(8,128)(2,1)S(1)}, bf16[2,2,128,128]{3,2,1,0:T(8,128)(2,1)S(1)}, u32[]{:S(2)}, u32[]{:S(2)}) collective-permute-start(bf16[2,2,128,128]{3,2,1,0:T(8,128)(2,1)S(1)} %bitcast.125), channel_id=1, source_target_pairs={{0,4},{4,0},{8,12},{12,8},{16,20},{20,16},{24,28},{28,24},{1,5},{5... | collective-permute-start | bytes 393224 | tf_op jit(solution)/shard_map/ppermute | solution.py:25
  98.1 2.6 %scatter-add.9 = f32[2,2,2,64,128]{4,2,3,1,0:T(2,128)S(1)} dynamic-update-slice(f32[2,2,2,64,128]{4,2,3,1,0:T(2,128)S(1)} %copy.62, f32[2,2,1,64,128]{4,2,3,1,0:T(1,128)S(1)} %add.68, s32[]{:T(128)} %constant.122.clone.1, s32[]{:T(128)} %constant.122.clone.1, s32[]{:T(128)} %constant.126.clone.1, s32[]{:T(128)} %constant.122.clone.1, s32[]{:T(128)} %constant.122.clone.1) | dynamic-update-slice | bytes 262148 | tf_op jit(solution)/shard_map/scatter-add | solution.py:139
  100.9 0.9 collective-permute-done.14
  101.9 1.2 collective-permute-start.15
  104.2 4.2 %collective-permute-done.18 = bf16[2,2,128,128]{3,2,1,0:T(8,128)(2,1)S(1)} collective-permute-done((bf16[2,2,128,128]{3,2,1,0:T(8,128)(2,1)S(1)}, bf16[2,2,128,128]{3,2,1,0:T(8,128)(2,1)S(1)}, u32[]{:S(2)}, u32[]{:S(2)}) %collective-permute-start.18) | collective-permute-done | bytes 131104 | tf_op jit(solution)/shard_map/ppermute | solution.py:25
  108.5 1.4 collective-permute-done.15
  110.0 1.5 collective-permute-start.16
  111.7 1.5 collective-permute-start.13
  113.2 4.5 %collective-permute-done.19 = bf16[2,2,128,128]{3,2,1,0:T(8,128)(2,1)S(1)} collective-permute-done((bf16[2,2,128,128]{3,2,1,0:T(8,128)(2,1)S(1)}, bf16[2,2,128,128]{3,2,1,0:T(8,128)(2,1)S(1)}, u32[]{:S(2)}, u32[]{:S(2)}) %collective-permute-start.19) | collective-permute-done | bytes 131104 | tf_op jit(solution)/shard_map/ppermute | solution.py:25
  117.7 1.6 collective-permute-done.16
  119.4 1.4 collective-permute-done.13
  121.0 43.2 %all-reduce.6.cloned.1.call-done = f32[2,2,2,64,128]{4,2,3,1,0:T(2,128)} async-done(((f32[2,2,2,64,128]{4,2,3,1,0:T(2,128)}), f32[2,2,2,64,128]{4,2,3,1,0:T(2,128)}) %all-reduce.6.cloned.1.call-update) | async-done | bytes 262160 | tf_op jit(solution)/shard_map/psum | solution.py:143
  164.1 1.8 %fusion.7 = bf16[2,2,2,64,128]{4,2,3,1,0:T(2,128)(2,1)S(1)} fusion(f32[2,2,2,64,128]{4,2,3,1,0:T(2,128)S(1)} %scatter-add.9, f32[2,2,2,64,128]{4,2,3,1,0:T(2,128)} %all-reduce.6.cloned.1.call-done, f32[2,2,2,64,128]{4,3,2,1,0:T(8,128)S(1)} %bitcast.136, pred[2]{0:T(512)(128)(4,1)S(1)} %get-tuple-element.63, s32[2]{0:T(128)S(1)} %get-tuple-element.39), kind=kOutput, calls=%fused_computation.14 | convolution fusion | flops 1769480 | bytes 917514 | tf_op jit(solution)/shard_map/gn,chgbd->chnbd/dot_general | solution.py:147
  (106 shorter events, 13.1 us)
Async XLA Ops:
  7.2 74.9 %copy-start = (bf16[2,128,128]{2,1,0:T(8,128)(2,1)S(1)}, bf16[2,128,128]{2,1,0:T(8,128)(2,1)}, u32[]{:S(2)}) copy-start(bf16[2,128,128]{2,1,0:T(8,128)(2,1)} %param.10) | copy-start | bytes 196612
  7.2 157.0 %all-reduce.6.cloned.1.call-start = ((), (), s32[]{:S(2)}) async-start(), calls=%async_computation | async-start | bytes 524288 | tf_op jit(solution)/shard_map/psum | solution.py:143
  7.2 7.7 %copy-start.1 = (bf16[2,128,128]{2,1,0:T(8,128)(2,1)S(1)}, bf16[2,128,128]{2,1,0:T(8,128)(2,1)}, u32[]{:S(2)}) copy-start(bf16[2,128,128]{2,1,0:T(8,128)(2,1)} %param.11) | copy-start | bytes 196612
  7.2 7.7 %copy-start.2 = (bf16[2,128,128]{2,1,0:T(8,128)(2,1)S(1)}, bf16[2,128,128]{2,1,0:T(8,128)(2,1)}, u32[]{:S(2)}) copy-start(bf16[2,128,128]{2,1,0:T(8,128)(2,1)} %param.12) | copy-start | bytes 196612
  8.1 51.4 %collective-permute-start.1 = (bf16[2,2,64,128]{3,2,1,0:T(8,128)(2,1)S(1)}, bf16[2,2,64,128]{3,2,1,0:T(8,128)(2,1)S(1)}, u32[]{:S(2)}, u32[]{:S(2)}) collective-permute-start(bf16[2,2,64,128]{3,2,1,0:T(8,128)(2,1)S(1)} %get-tuple-element.61), channel_id=1, source_target_pairs={{4,0},{8,4},{12,8},{16,12},{20,16},{24,20},{28,24},{5,1},{9,5},{13... | collective-permute-start | bytes 196616 | tf_op jit(solution)/shard_map/ppermute | solution.py:17
  9.4 50.1 %collective-permute-start = (bf16[2,2,64,128]{3,2,1,0:T(8,128)(2,1)S(1)}, bf16[2,2,64,128]{3,2,1,0:T(8,128)(2,1)S(1)}, u32[]{:S(2)}, u32[]{:S(2)}) collective-permute-start(bf16[2,2,64,128]{3,2,1,0:T(8,128)(2,1)S(1)} %get-tuple-element.60), channel_id=1, source_target_pairs={{0,4},{4,8},{8,12},{12,16},{16,20},{20,24},{24,28},{1,5},{5,9},{9,... | collective-permute-start | bytes 196616 | tf_op jit(solution)/shard_map/ppermute | solution.py:16
  15.0 3.0 %copy-start.4 = (s32[2,2,3]{2,1,0:T(2,128)S(1)}, s32[2,2,3]{2,1,0:T(2,128)}, u32[]{:S(2)}) copy-start(s32[2,2,3]{2,1,0:T(2,128)} %param.14) | copy-start | bytes 148
  15.0 45.0 %collective-permute-start.2 = (bf16[2,2,128,128]{3,2,1,0:T(8,128)(2,1)S(1)}, bf16[2,2,128,128]{3,2,1,0:T(8,128)(2,1)S(1)}, u32[]{:S(2)}, u32[]{:S(2)}) collective-permute-start(bf16[2,2,128,128]{3,2,1,0:T(8,128)(2,1)S(1)} %pad_maximum_fusion.7), channel_id=1, source_target_pairs={{0,4},{4,0},{8,12},{12,8},{16,20},{20,16},{24,28},{28,24},{1,5},{5... | collective-permute-start | bytes 393224 | tf_op jit(solution)/shard_map/ppermute | solution.py:25
  18.0 0.7 copy-start.5
  58.0 0.7 slice-start
  60.2 6.4 %collective-permute-start.7 = (bf16[2,2,128,128]{3,2,1,0:T(8,128)(2,1)S(1)}, bf16[2,2,128,128]{3,2,1,0:T(8,128)(2,1)S(1)}, u32[]{:S(2)}, u32[]{:S(2)}) collective-permute-start(bf16[2,2,128,128]{3,2,1,0:T(8,128)(2,1)S(1)} %get-tuple-element.53), channel_id=1, source_target_pairs={{0,8},{4,12},{8,0},{12,4},{16,24},{20,28},{24,16},{28,20},{1,9},{5... | collective-permute-start | bytes 393224 | tf_op jit(solution)/shard_map/ppermute | solution.py:25
  60.4 9.2 %collective-permute-start.5 = (bf16[2,2,128,128]{3,2,1,0:T(8,128)(2,1)S(1)}, bf16[2,2,128,128]{3,2,1,0:T(8,128)(2,1)S(1)}, u32[]{:S(2)}, u32[]{:S(2)}) collective-permute-start(bf16[2,2,128,128]{3,2,1,0:T(8,128)(2,1)S(1)} %get-tuple-element.54), channel_id=1, source_target_pairs={{0,8},{4,12},{8,0},{12,4},{16,24},{20,28},{24,16},{28,20},{1,9},{5... | collective-permute-start | bytes 393224 | tf_op jit(solution)/shard_map/ppermute | solution.py:25
  62.5 8.6 %collective-permute-start.3 = (bf16[2,2,128,128]{3,2,1,0:T(8,128)(2,1)S(1)}, bf16[2,2,128,128]{3,2,1,0:T(8,128)(2,1)S(1)}, u32[]{:S(2)}, u32[]{:S(2)}) collective-permute-start(bf16[2,2,128,128]{3,2,1,0:T(8,128)(2,1)S(1)} %get-tuple-element.52), channel_id=1, source_target_pairs={{0,8},{4,12},{8,0},{12,4},{16,24},{20,28},{24,16},{28,20},{1,9},{5... | collective-permute-start | bytes 393224 | tf_op jit(solution)/shard_map/ppermute | solution.py:25
  66.7 9.6 %collective-permute-start.8 = (bf16[2,2,128,128]{3,2,1,0:T(8,128)(2,1)S(1)}, bf16[2,2,128,128]{3,2,1,0:T(8,128)(2,1)S(1)}, u32[]{:S(2)}, u32[]{:S(2)}) collective-permute-start(bf16[2,2,128,128]{3,2,1,0:T(8,128)(2,1)S(1)} %broadcast_select_fusion.3), channel_id=1, source_target_pairs={{0,16},{4,20},{8,24},{12,28},{16,0},{20,4},{24,8},{28,12},{1,17},{... | collective-permute-start | bytes 393224 | tf_op jit(solution)/shard_map/ppermute | solution.py:25
  69.7 8.4 %collective-permute-start.6 = (bf16[2,2,128,128]{3,2,1,0:T(8,128)(2,1)S(1)}, bf16[2,2,128,128]{3,2,1,0:T(8,128)(2,1)S(1)}, u32[]{:S(2)}, u32[]{:S(2)}) collective-permute-start(bf16[2,2,128,128]{3,2,1,0:T(8,128)(2,1)S(1)} %broadcast_select_fusion.8), channel_id=1, source_target_pairs={{0,16},{4,20},{8,24},{12,28},{16,0},{20,4},{24,8},{28,12},{1,17},{... | collective-permute-start | bytes 393224 | tf_op jit(solution)/shard_map/ppermute | solution.py:25
  71.2 8.6 %collective-permute-start.4 = (bf16[2,2,128,128]{3,2,1,0:T(8,128)(2,1)S(1)}, bf16[2,2,128,128]{3,2,1,0:T(8,128)(2,1)S(1)}, u32[]{:S(2)}, u32[]{:S(2)}) collective-permute-start(bf16[2,2,128,128]{3,2,1,0:T(8,128)(2,1)S(1)} %broadcast_select_fusion.13), channel_id=1, source_target_pairs={{0,16},{4,20},{8,24},{12,28},{16,0},{20,4},{24,8},{28,12},{1,17},{... | collective-permute-start | bytes 393224 | tf_op jit(solution)/shard_map/ppermute | solution.py:25
  82.4 0.8 copy-start.3
  86.1 11.6 %collective-permute-start.10 = (bf16[2,2,64,128]{3,2,1,0:T(8,128)(2,1)S(1)}, bf16[2,2,64,128]{3,2,1,0:T(8,128)(2,1)S(1)}, u32[]{:S(2)}, u32[]{:S(2)}) collective-permute-start(bf16[2,2,64,128]{3,2,1,0:T(8,128)(2,1)S(1)} %get-tuple-element.51), channel_id=1, source_target_pairs={{4,0},{8,4},{12,8},{16,12},{20,16},{24,20},{28,24},{5,1},{9,5},{13... | collective-permute-start | bytes 196616 | tf_op jit(solution)/shard_map/ppermute | solution.py:17
  87.4 10.3 %collective-permute-start.9 = (bf16[2,2,64,128]{3,2,1,0:T(8,128)(2,1)S(1)}, bf16[2,2,64,128]{3,2,1,0:T(8,128)(2,1)S(1)}, u32[]{:S(2)}, u32[]{:S(2)}) collective-permute-start(bf16[2,2,64,128]{3,2,1,0:T(8,128)(2,1)S(1)} %get-tuple-element.50), channel_id=1, source_target_pairs={{0,4},{4,8},{8,12},{12,16},{16,20},{20,24},{24,28},{1,5},{5,9},{9,... | collective-permute-start | bytes 196616 | tf_op jit(solution)/shard_map/ppermute | solution.py:16
  95.4 5.4 %collective-permute-start.17 = (bf16[2,2,128,128]{3,2,1,0:T(8,128)(2,1)S(1)}, bf16[2,2,128,128]{3,2,1,0:T(8,128)(2,1)S(1)}, u32[]{:S(2)}, u32[]{:S(2)}) collective-permute-start(bf16[2,2,128,128]{3,2,1,0:T(8,128)(2,1)S(1)} %bitcast.127), channel_id=1, source_target_pairs={{0,4},{4,0},{8,12},{12,8},{16,20},{20,16},{24,28},{28,24},{1,5},{5... | collective-permute-start | bytes 393224 | tf_op jit(solution)/shard_map/ppermute | solution.py:25
  95.5 6.3 %collective-permute-start.14 = (bf16[2,2,128,128]{3,2,1,0:T(8,128)(2,1)S(1)}, bf16[2,2,128,128]{3,2,1,0:T(8,128)(2,1)S(1)}, u32[]{:S(2)}, u32[]{:S(2)}) collective-permute-start(bf16[2,2,128,128]{3,2,1,0:T(8,128)(2,1)S(1)} %bitcast.125), channel_id=1, source_target_pairs={{0,4},{4,0},{8,12},{12,8},{16,20},{20,16},{24,28},{28,24},{1,5},{5... | collective-permute-start | bytes 393224 | tf_op jit(solution)/shard_map/ppermute | solution.py:25
  97.6 5.6 %collective-permute-start.11 = (bf16[2,2,128,128]{3,2,1,0:T(8,128)(2,1)S(1)}, bf16[2,2,128,128]{3,2,1,0:T(8,128)(2,1)S(1)}, u32[]{:S(2)}, u32[]{:S(2)}) collective-permute-start(bf16[2,2,128,128]{3,2,1,0:T(8,128)(2,1)S(1)} %bitcast.123), channel_id=1, source_target_pairs={{0,4},{4,0},{8,12},{12,8},{16,20},{20,16},{24,28},{28,24},{1,5},{5... | collective-permute-start | bytes 393224 | tf_op jit(solution)/shard_map/ppermute | solution.py:25
  100.9 7.5 %collective-permute-start.18 = (bf16[2,2,128,128]{3,2,1,0:T(8,128)(2,1)S(1)}, bf16[2,2,128,128]{3,2,1,0:T(8,128)(2,1)S(1)}, u32[]{:S(2)}, u32[]{:S(2)}) collective-permute-start(bf16[2,2,128,128]{3,2,1,0:T(8,128)(2,1)S(1)} %broadcast_select_fusion), channel_id=1, source_target_pairs={{0,8},{4,12},{8,0},{12,4},{16,24},{20,28},{24,16},{28,20},{1,9},{5... | collective-permute-start | bytes 393224 | tf_op jit(solution)/shard_map/ppermute | solution.py:25
  101.9 8.0 %collective-permute-start.15 = (bf16[2,2,128,128]{3,2,1,0:T(8,128)(2,1)S(1)}, bf16[2,2,128,128]{3,2,1,0:T(8,128)(2,1)S(1)}, u32[]{:S(2)}, u32[]{:S(2)}) collective-permute-start(bf16[2,2,128,128]{3,2,1,0:T(8,128)(2,1)S(1)} %broadcast_select_fusion.5), channel_id=1, source_target_pairs={{0,8},{4,12},{8,0},{12,4},{16,24},{20,28},{24,16},{28,20},{1,9},{5... | collective-permute-start | bytes 393224 | tf_op jit(solution)/shard_map/ppermute | solution.py:25
  103.3 8.2 %collective-permute-start.12 = (bf16[2,2,128,128]{3,2,1,0:T(8,128)(2,1)S(1)}, bf16[2,2,128,128]{3,2,1,0:T(8,128)(2,1)S(1)}, u32[]{:S(2)}, u32[]{:S(2)}) collective-permute-start(bf16[2,2,128,128]{3,2,1,0:T(8,128)(2,1)S(1)} %broadcast_select_fusion.10), channel_id=1, source_target_pairs={{0,8},{4,12},{8,0},{12,4},{16,24},{20,28},{24,16},{28,20},{1,9},{5... | collective-permute-start | bytes 393224 | tf_op jit(solution)/shard_map/ppermute | solution.py:25
  108.4 9.2 %collective-permute-start.19 = (bf16[2,2,128,128]{3,2,1,0:T(8,128)(2,1)S(1)}, bf16[2,2,128,128]{3,2,1,0:T(8,128)(2,1)S(1)}, u32[]{:S(2)}, u32[]{:S(2)}) collective-permute-start(bf16[2,2,128,128]{3,2,1,0:T(8,128)(2,1)S(1)} %broadcast_select_fusion.2), channel_id=1, source_target_pairs={{0,16},{4,20},{8,24},{12,28},{16,0},{20,4},{24,8},{28,12},{1,17},{... | collective-permute-start | bytes 393224 | tf_op jit(solution)/shard_map/ppermute | solution.py:25
  110.0 9.3 %collective-permute-start.16 = (bf16[2,2,128,128]{3,2,1,0:T(8,128)(2,1)S(1)}, bf16[2,2,128,128]{3,2,1,0:T(8,128)(2,1)S(1)}, u32[]{:S(2)}, u32[]{:S(2)}) collective-permute-start(bf16[2,2,128,128]{3,2,1,0:T(8,128)(2,1)S(1)} %broadcast_select_fusion.7), channel_id=1, source_target_pairs={{0,16},{4,20},{8,24},{12,28},{16,0},{20,4},{24,8},{28,12},{1,17},{... | collective-permute-start | bytes 393224 | tf_op jit(solution)/shard_map/ppermute | solution.py:25
  111.7 9.1 %collective-permute-start.13 = (bf16[2,2,128,128]{3,2,1,0:T(8,128)(2,1)S(1)}, bf16[2,2,128,128]{3,2,1,0:T(8,128)(2,1)S(1)}, u32[]{:S(2)}, u32[]{:S(2)}) collective-permute-start(bf16[2,2,128,128]{3,2,1,0:T(8,128)(2,1)S(1)} %broadcast_select_fusion.12), channel_id=1, source_target_pairs={{0,16},{4,20},{8,24},{12,28},{16,0},{20,4},{24,8},{28,12},{1,17},{... | collective-permute-start | bytes 393224 | tf_op jit(solution)/shard_map/ppermute | solution.py:25
Sparse Core Ops, SparseCore 0:
  93.2 70.8 all-reduce.5
where the time goes:
time: 175 us; the launch traced here: 174 us
  waiting for transfers between devices  71.9 us (41%)
  blocking collectives  38.6 us (22%)
  starting transfers between devices  27.4 us (16%)
  between operations  14.6 us (8%)
  local copies, waits for them, and re-layouts  10.8 us (6%)
  matrix products  7.31 us (4%)
  other arithmetic  3.48 us (2%)
    psum x1, waiting for transfers between devices, on_device(): global_total = lax.psum(global_part, 'seq')  43.2 us
    psum x1, blocking collectives, on_device(): global_sum = lax.psum(picked * owned[None, None, :, None, None], 'seq')  38.6 us
    ppermute x16, waiting for transfers between devices, swapped(): return lax.ppermute(value, axis, pairs)  28.7 us
    ppermute x16, starting transfers between devices, swapped(): return lax.ppermute(value, axis, pairs)  14.5 us
    ppermute x2, starting transfers between devices, with_halo(): before = lax.ppermute(last, axis, up)  10.3 us
  transfers between devices with their start and end apart: 21, of which 14 were waited for; matrix products, arithmetic and copies ran while one was open for 6% of the time, Pallas kernels for 0%

commit v1 on v0

--- a/solution.py
+++ b/solution.py
@@ -1,9 +1,189 @@
+import functools
 import math
 
 import jax
 import jax.numpy as jnp
 from jax import lax
+from jax.experimental import pallas as pl
+from jax.experimental.pallas import tpu as pltpu
 from jax.sharding import PartitionSpec as P
+
+GATHER_BYTES = 8 * 2**20
+LOG2E = math.log2(math.e)
+
+
+def ring_order(count):
+    return list(range(0, count, 2)) + list(range(1, count, 2))[::-1]
+
+
+def dense_kernel(sizes, *refs):
+    heads, shards, rows, width, block_rows, slots = sizes
+    nk_ref, gcount_ref = refs[0], refs[1]
+    a_refs = refs[2 : 2 + shards]
+    b_refs = refs[2 + shards : 2 + 2 * shards]
+    dq_ref, dk_ref, dv_ref = refs[2 + 2 * shards : 5 + 2 * shards]
+    kv, qg, head_buf, ids, bias, s_buf, e_buf, p_buf, sems = refs[5 + 2 * shards :]
+    total = shards * rows
+    key_blocks = total // block_rows
+    own_blocks = rows // block_rows
+    scale = 1.0 / math.sqrt(width)
+    rate = scale * LOG2E
+    copies = []
+    for s in range(shards):
+        for part in range(2 * heads):
+            copies.append(
+                pltpu.make_async_copy(
+                    a_refs[s].at[pl.ds(part * rows, rows)],
+                    kv.at[part, pl.ds(s * rows, rows)],
+                    sems.at[0],
+                )
+            )
+            copies.append(
+                pltpu.make_async_copy(
+                    b_refs[s].at[pl.ds(part * rows, rows)],
+                    qg.at[part, pl.ds(s * rows, rows)],
+                    sems.at[0],
+                )
+            )
+        copies.append(
+            pltpu.make_async_copy(
+                a_refs[s].at[pl.ds(2 * heads * rows, head_buf.shape[1])], head_buf.at[s], sems.at[0]
+            )
+        )
+    for c in copies:
+        c.start()
+    for c in copies:
+        c.wait()
+    for s in range(shards):
+        ids[:, s * rows : (s + 1) * rows] = head_buf[s].astype(jnp.float32)
+    nk = nk_ref[...]
+    gcount = gcount_ref[...]
+    last = heads * slots
+    for h in range(heads):
+        for s in range(shards):
+            lanes = slice(s * rows, (s + 1) * rows)
+            nq = ids[last : last + 1, lanes]
+            count = gcount + jnp.where(jnp.abs(nk - nq) <= 1.0, 1.0, 0.0)
+            for j in range(slots):
+                rid = ids[h * slots + j : h * slots + j + 1, lanes]
+                count = count + jnp.where(nk == rid, 1.0, 0.0)
+            bias[h, :, lanes] = jnp.where(
+                count > 0.5, jnp.log(jnp.maximum(count, 1.0)) * (1.0 / scale), -1e30
+            )
+    dk = [jnp.zeros((rows, width), jnp.float32) for _ in range(heads)]
+    dv = [jnp.zeros((rows, width), jnp.float32) for _ in range(heads)]
+    pair = 2 * rows
+    nt = (((1,), (1,)), ((), ()))
+    for pi in range(shards // 2):
+        lanes = slice(pi * pair, (pi + 1) * pair)
+        for h in range(heads):
+            q = qg[h, lanes]
+            g = qg[heads + h, lanes]
+            s_buf[h, 0] = lax.dot_general(kv[h], q, nt, preferred_element_type=jnp.float32)
+            s_buf[h, 1] = lax.dot_general(kv[heads + h], g, nt, preferred_element_type=jnp.float32)
+            top = jnp.full((8, pair), -1e30, jnp.float32)
+            for kb in range(key_blocks):
+                x = s_buf[h, 0, kb * block_rows : (kb + 1) * block_rows] + bias[h, kb : kb + 1, lanes]
+                top = jnp.maximum(top, jnp.max(x.reshape(block_rows // 8, 8, pair), axis=0))
+            top = jnp.max(top, axis=0, keepdims=True)
+            acc_l = jnp.zeros((8, pair), jnp.float32)
+            acc_d = jnp.zeros((8, pair), jnp.float32)
+            for kb in range(key_blocks):
+                rws = slice(kb * block_rows, (kb + 1) * block_rows)
+                shift = (bias[h, kb : kb + 1, lanes] - top) * rate
+                e = jnp.exp2(s_buf[h, 0, rws] * rate + shift)
+                d = e * s_buf[h, 1, rws]
+                acc_l = acc_l + jnp.sum(e.reshape(block_rows // 8, 8, pair), axis=0)
+                acc_d = acc_d + jnp.sum(d.reshape(block_rows // 8, 8, pair), axis=0)
+                if kb < own_blocks:
+                    e_buf[h, rws] = e
+                elif pi == 0:
+                    e_buf[h, rws, 0:rows] = e[:, 0:rows]
+            inv = 1.0 / jnp.sum(acc_l, axis=0, keepdims=True)
+            dot_row = jnp.sum(acc_d, axis=0, keepdims=True) * inv
+            p_own = e_buf[h, 0:rows] * inv
+            ds_own = p_own * (s_buf[h, 1, 0:rows] - dot_row)
+            dv[h] = dv[h] + jnp.dot(p_own.astype(jnp.bfloat16), g, preferred_element_type=jnp.float32)
+            dk[h] = dk[h] + jnp.dot(ds_own.astype(jnp.bfloat16), q, preferred_element_type=jnp.float32)
+            if pi == 0:
+                for kb in range(key_blocks):
+                    rws = slice(kb * block_rows, (kb + 1) * block_rows)
+                    ds = e_buf[h, rws, 0:rows] * inv[:, 0:rows]
+                    ds = ds * (s_buf[h, 1, rws, 0:rows] - dot_row[:, 0:rows])
+                    p_buf[h, rws] = ds.astype(jnp.bfloat16)
+                dq = lax.dot_general(
+                    p_buf[h], kv[h], (((0,), (0,)), ((), ())), preferred_element_type=jnp.float32
+                )
+                dq_ref[h] = (dq * scale).astype(dq_ref.dtype)
+    for h in range(heads):
+        dk_ref[h] = (dk[h] * scale).astype(dk_ref.dtype)
+        dv_ref[h] = dv[h].astype(dv_ref.dtype)
+
+
+def gathered(queries, keys, values, grad_out, rand_ids, global_ids):
+    heads, rows, width = queries.shape
+    blocks, slots = rand_ids.shape[1:]
+    block_rows = rows // blocks
+    count = lax.axis_size("seq")
+    me = lax.axis_index("seq")
+    ring = ring_order(count)
+    place = [ring.index(i) for i in range(count)]
+    forward = [(ring[i], ring[(i + 1) % count]) for i in range(count)]
+    backward = [(b, a) for a, b in forward]
+    half = count // 2
+    steps = [0]
+    for d in range(1, half):
+        steps += [-d, d]
+    steps.append(half)
+    my_place = jnp.asarray(place, jnp.int32)[me]
+    owners = jnp.asarray(ring, jnp.int32)[(my_place + jnp.asarray(steps, jnp.int32)) % count]
+    nk = (owners[:, None] * blocks + jnp.arange(blocks, dtype=jnp.int32)[None]).reshape(-1, 1)
+    gcount = jnp.sum((nk == global_ids[None, :]).astype(jnp.float32), axis=1, keepdims=True)
+    nk = jnp.broadcast_to(nk.astype(jnp.float32), (count * blocks, rows))
+    gcount = jnp.broadcast_to(gcount, (count * blocks, rows))
+
+    token_ids = jnp.repeat(jnp.moveaxis(rand_ids, 2, 1).reshape(heads * slots, blocks), block_rows, axis=1)
+    mine = me * blocks + jnp.arange(rows, dtype=jnp.int32)[None] // block_rows
+    head_rows = -(-(heads * slots + 1) // 16) * 16
+    header = jnp.concatenate(
+        [token_ids, mine, jnp.zeros((head_rows - heads * slots - 1, rows), jnp.int32)]
+    ).astype(jnp.bfloat16)
+    flat = lambda x: x.reshape(heads * rows, width)
+    a = jnp.concatenate([flat(keys), flat(values), header])
+    b = jnp.concatenate([flat(queries), flat(grad_out)])
+    a_all, b_all = [a], [b]
+    af = ab = a
+    bf = bb = b
+    for _ in range(1, half):
+        af, ab = lax.ppermute(af, "seq", forward), lax.ppermute(ab, "seq", backward)
+        bf, bb = lax.ppermute(bf, "seq", forward), lax.ppermute(bb, "seq", backward)
+        a_all += [af, ab]
+        b_all += [bf, bb]
+    a_all.append(lax.ppermute(af, "seq", forward))
+    b_all.append(lax.ppermute(bb, "seq", backward))
+
+    sizes = (heads, count, rows, width, block_rows, slots)
+    total = count * rows
+    out = jax.ShapeDtypeStruct(queries.shape, queries.dtype)
+    vmem = pl.BlockSpec(memory_space=pltpu.VMEM)
+    anyspace = pl.BlockSpec(memory_space=pl.ANY)
+    return pl.pallas_call(
+        functools.partial(dense_kernel, sizes),
+        out_shape=(out, out, out),
+        in_specs=[vmem, vmem] + [anyspace] * (2 * count),
+        out_specs=(vmem, vmem, vmem),
+        scratch_shapes=[
+            pltpu.VMEM((2 * heads, total, width), jnp.bfloat16),
+            pltpu.VMEM((2 * heads, total, width), jnp.bfloat16),
+            pltpu.VMEM((count, head_rows, rows), jnp.bfloat16),
+            pltpu.VMEM((head_rows, total), jnp.float32),
+            pltpu.VMEM((heads, count * blocks, total), jnp.float32),
+            pltpu.VMEM((heads, 2, total, 2 * rows), jnp.float32),
+            pltpu.VMEM((heads, total, 2 * rows), jnp.float32),
+            pltpu.VMEM((heads, total, rows), jnp.bfloat16),
+            pltpu.SemaphoreType.DMA((1,)),
+        ],
+    )(nk, gcount, *a_all, *b_all)
 
 
 def with_halo(value, sides, width):
@@ -29,7 +209,7 @@
     return list(range(section_count))
 
 
-def on_device(queries, keys, values, grad_out, rand_ids, global_ids):
+def routed(queries, keys, values, grad_out, rand_ids, global_ids):
     head_count, row_count, head_width = queries.shape
     block_count = rand_ids.shape[1]
     slot_count = rand_ids.shape[2]
@@ -174,6 +354,15 @@
     return (grad_queries, grad_keys, grad_values)
 
 
+def on_device(queries, keys, values, grad_out, rand_ids, global_ids):
+    count = lax.axis_size("seq")
+    rows, width = queries.shape[1:]
+    gathered_bytes = 4 * count * queries.size * queries.dtype.itemsize
+    if gathered_bytes <= GATHER_BYTES and count % 2 == 0 and rows == width:
+        return gathered(queries, keys, values, grad_out, rand_ids, global_ids)
+    return routed(queries, keys, values, grad_out, rand_ids, global_ids)
+
+
 def solution(mesh):
     in_specs = (
         P("head", "seq", None),

time: 175 us -> 43.3 us (0.25)
  waiting for transfers between devices: 71.9 us -> 9.85 us
  blocking collectives: 38.6 us -> 0 us
  between operations: 14.6 us -> 0.86 us
  starting transfers between devices: 27.4 us -> 15.5 us
  Pallas kernels: 0 us -> 8.81 us
  matrix products: 7.31 us -> 0 us
  local copies, waits for them, and re-layouts: 10.8 us -> 6.92 us
  other arithmetic: 3.48 us -> 0.86 us
    psum x1 -> x0, waiting for transfers between devices: 43.2 us -> none  [on_device(): global_total = lax.psum(global_part, 'seq')]
    psum x1 -> x0, blocking collectives: 38.6 us -> none  [on_device(): global_sum = lax.psum(picked * owned[None, None, :, None, None], 'seq')]
    ppermute x20 -> x14, waiting for transfers between devices: 28.7 us -> 9.85 us  [the longest x3 5.67 us: gathered(): lax.ppermute(bb, 'seq', backward)]
    ppermute x20 -> x14, starting transfers between devices: 27.4 us -> 15.5 us  [the longest x3 7.01 us: gathered(): lax.ppermute(af, 'seq', forward)]
    pallas_call x0 -> x1, Pallas kernels: none -> 8.81 us  [gathered(): pl.pallas_call(functools.partial(dense_kernel, sizes), out_shape=(out, ou...]
    dot_general x9 -> x0, matrix products: 7.31 us -> none  [the longest x1 1.94 us: on_device(): jnp.einsum('hqjl,chqjbd->jchlbd', local_float, random_part, precision=lax...]
    slice x12 -> x0, local copies, waits for them, and re-layouts: 3.75 us -> none  [the longest x1 1.24 us: on_device(): all_keys[0]]
    scatter-add x2 -> x0, local copies, waits for them, and re-layouts: 2.83 us -> none  [the longest x1 2.62 us: on_device(): own_grads.at[:, :, block_count - 1]]
  transfers between devices with their start and end apart: 21 -> 14, of which waited for: 14 -> 6; matrix products, arithmetic and copies ran while one was open for 6% -> 5% of each run, Pallas kernels for 0% -> 0%
where the time goes in v1:
time: 43.3 us; the launch traced here: 42.9 us
  starting transfers between devices  15.5 us (36%)
  waiting for transfers between devices  9.85 us (23%)
  Pallas kernels  8.81 us (20%)
  local copies, waits for them, and re-layouts  6.92 us (16%)
  other arithmetic  0.86 us (2%)
  between operations  0.86 us (2%)
    pallas_call x1, Pallas kernels, gathered(): pl.pallas_call(functools.partial(dense_kernel, sizes), out_shape=(out, ou...  8.81 us
    ppermute x3, starting transfers between devices, gathered(): lax.ppermute(af, 'seq', forward)  7.01 us
    ppermute x3, waiting for transfers between devices, gathered(): lax.ppermute(bb, 'seq', backward)  5.67 us
    ppermute x3, starting transfers between devices, gathered(): lax.ppermute(bf, 'seq', forward)  5.54 us
    unnamed x46, local copies, waits for them, and re-layouts  2.04 us
    ppermute x1, waiting for transfers between devices, gathered(): b_all.append(lax.ppermute(bb, 'seq', backward))  2.01 us
    concatenate x1, local copies, waits for them, and re-layouts, gathered(): a = jnp.concatenate([flat(keys), flat(values), header])  1.88 us
    ppermute x3, waiting for transfers between devices, gathered(): lax.ppermute(bf, 'seq', forward)  1.72 us
  transfers between devices with their start and end apart: 14, of which 6 were waited for; matrix products, arithmetic and copies ran while one was open for 5% of the time, Pallas kernels for 0%

profile of v1, /device:TPU:0, one launch (start us, length us, event | category | flops | bytes accessed | tf_op | source)
XLA Modules:
  0.0 42.9 jit_solution(10893388945210961709)
XLA Ops:
  0.7 0.7 %copy-done.19 = s32[2,2,3]{2,1,0:T(2,128)S(1)} copy-done((s32[2,2,3]{2,1,0:T(2,128)S(1)}, s32[2,2,3]{2,1,0:T(2,128)}, u32[]{:S(2)}) %copy-start.19) | copy-done | bytes 72
  1.3 0.1 reshape.125
  1.4 0.1 copy.17
  1.6 0.1 reshape.122
  1.7 1.9 %concatenate.9.refs_2_ = bf16[528,128]{1,0:T(8,128)(2,1)S(1)} concatenate(bf16[256,128]{1,0:T(8,128)(2,1)} %bitcast.9, bf16[256,128]{1,0:T(8,128)(2,1)} %bitcast.10, bf16[6,128]{1,0:T(8,128)(2,1)S(1)} %reshape.122, bf16[1,128]{1,0:T(2,128)(2,1)S(1)} %fusion.3, bf16[9,128]{1,0:T(8,128)(2,1)S(1)} %broadcast_in_dim.28), dimensions={0} | concatenate | bytes 270336 | tf_op jit(solution)/shard_map/concatenate | solution.py:152
  3.6 3.1 %collective-permute-start = (bf16[528,128]{1,0:T(8,128)(2,1)S(1)}, bf16[528,128]{1,0:T(8,128)(2,1)S(1)}, u32[]{:S(2)}, u32[]{:S(2)}) collective-permute-start(bf16[528,128]{1,0:T(8,128)(2,1)S(1)} %concatenate.9.refs_2_), channel_id=1, source_target_pairs={{0,8},{8,16},{16,24},{24,28},{28,20},{20,12},{12,4},{4,0},{1,9},{9... | collective-permute-start | bytes 405512 | tf_op jit(solution)/shard_map/ppermute | solution.py:158
  6.8 2.0 %collective-permute-start.7 = (bf16[512,128]{1,0:T(8,128)(2,1)S(1)}, bf16[512,128]{1,0:T(8,128)(2,1)S(1)}, u32[]{:S(2)}, u32[]{:S(2)}) collective-permute-start(bf16[512,128]{1,0:T(8,128)(2,1)S(1)} %pad_maximum_fusion.refs_10_), channel_id=1, source_target_pairs={{0,8},{8,16},{16,24},{24,28},{28,20},{20,12},{12,4},{4,0},{1,9},{9... | collective-permute-start | bytes 393224 | tf_op jit(solution)/shard_map/ppermute | solution.py:159
  8.9 0.7 %copy-done.22 = s32[8]{0:T(128)S(1)} copy-done((s32[8]{0:T(128)S(1)}, s32[8]{0:T(128)}, u32[]{:S(2)}) %copy-start.22) | copy-done | bytes 56
  9.5 0.6 %dynamic_slice.3 = s32[1]{0:T(128)} dynamic-slice(s32[8]{0:T(128)S(1)} %copy-done.22, s32[]{:T(128)S(6)} %select_n.26), dynamic_slice_sizes={1} | dynamic-slice | bytes 12 | tf_op jit(solution)/shard_map/dynamic_slice | solution.py:138
  10.1 3.0 %collective-permute-done.8.refs_12_ = bf16[512,128]{1,0:T(8,128)(2,1)S(1)} collective-permute-done((bf16[512,128]{1,0:T(8,128)(2,1)S(1)}, bf16[512,128]{1,0:T(8,128)(2,1)S(1)}, u32[]{:S(2)}, u32[]{:S(2)}) %collective-permute-start.8) | collective-permute-done | bytes 131104 | tf_op jit(solution)/shard_map/ppermute | solution.py:159
  13.2 2.0 %collective-permute-start.2 = (bf16[528,128]{1,0:T(8,128)(2,1)S(1)}, bf16[528,128]{1,0:T(8,128)(2,1)S(1)}, u32[]{:S(2)}, u32[]{:S(2)}) collective-permute-start(bf16[528,128]{1,0:T(8,128)(2,1)S(1)} %collective-permute-done.refs_3_), channel_id=1, source_target_pairs={{0,8},{8,16},{16,24},{24,28},{28,20},{20,12},{12,4},{4,0},{1,9},{9... | collective-permute-start | bytes 405512 | tf_op jit(solution)/shard_map/ppermute | solution.py:158
  15.1 0.7 %compare_select_fusion = s32[8]{0:T(128)S(1)} fusion(s32[8]{0:T(128)S(1)} %copy-done.21, s32[]{:T(128)} %bitcast), kind=kLoop, calls=%fused_computation.4 | loop fusion | flops 120 | bytes 68 | tf_op jit(solution)/shard_map/select_n | solution.py:139
  15.8 0.6 %gather_fusion = s32[8]{0:T(128)S(1)} fusion(s32[8]{0:T(128)S(1)} %copy-done, s32[1024]{0:T(1024)S(1)} %pad_clamp_fusion), kind=kCustom, calls=%fused_computation | custom fusion | bytes 96 | tf_op jit(solution)/shard_map/gather | solution.py:139
  16.5 1.6 %collective-permute-start.9 = (bf16[512,128]{1,0:T(8,128)(2,1)S(1)}, bf16[512,128]{1,0:T(8,128)(2,1)S(1)}, u32[]{:S(2)}, u32[]{:S(2)}) collective-permute-start(bf16[512,128]{1,0:T(8,128)(2,1)S(1)} %collective-permute-done.7.refs_11_), channel_id=1, source_target_pairs={{0,8},{8,16},{16,24},{24,28},{28,20},{20,12},{12,4},{4,0},{1,9},{9... | collective-permute-start | bytes 393224 | tf_op jit(solution)/shard_map/ppermute | solution.py:159
  18.2 0.4 %collective-permute-start.3 = (bf16[528,128]{1,0:T(8,128)(2,1)S(1)}, bf16[528,128]{1,0:T(8,128)(2,1)S(1)}, u32[]{:S(2)}, u32[]{:S(2)}) collective-permute-start(bf16[528,128]{1,0:T(8,128)(2,1)S(1)} %collective-permute-done.1.refs_4_), channel_id=1, source_target_pairs={{8,0},{16,8},{24,16},{28,24},{20,28},{12,20},{4,12},{0,4},{9,1},{1... | collective-permute-start | bytes 405512 | tf_op jit(solution)/shard_map/ppermute | solution.py:158
  18.6 0.3 collective-permute-done.10.refs_14_
  18.9 0.1 collective-permute-start.12
  19.0 1.9 %collective-permute-start.4 = (bf16[528,128]{1,0:T(8,128)(2,1)S(1)}, bf16[528,128]{1,0:T(8,128)(2,1)S(1)}, u32[]{:S(2)}, u32[]{:S(2)}) collective-permute-start(bf16[528,128]{1,0:T(8,128)(2,1)S(1)} %collective-permute-done.2.refs_5_), channel_id=1, source_target_pairs={{0,8},{8,16},{16,24},{24,28},{28,20},{20,12},{12,4},{4,0},{1,9},{9... | collective-permute-start | bytes 405512 | tf_op jit(solution)/shard_map/ppermute | solution.py:158
  20.9 1.7 %collective-permute-done.9.refs_13_ = bf16[512,128]{1,0:T(8,128)(2,1)S(1)} collective-permute-done((bf16[512,128]{1,0:T(8,128)(2,1)S(1)}, bf16[512,128]{1,0:T(8,128)(2,1)S(1)}, u32[]{:S(2)}, u32[]{:S(2)}) %collective-permute-start.9) | collective-permute-done | bytes 131104 | tf_op jit(solution)/shard_map/ppermute | solution.py:159
  22.6 1.9 %collective-permute-start.11 = (bf16[512,128]{1,0:T(8,128)(2,1)S(1)}, bf16[512,128]{1,0:T(8,128)(2,1)S(1)}, u32[]{:S(2)}, u32[]{:S(2)}) collective-permute-start(bf16[512,128]{1,0:T(8,128)(2,1)S(1)} %collective-permute-done.9.refs_13_), channel_id=1, source_target_pairs={{0,8},{8,16},{16,24},{24,28},{28,20},{20,12},{12,4},{4,0},{1,9},{9... | collective-permute-start | bytes 393224 | tf_op jit(solution)/shard_map/ppermute | solution.py:159
  24.5 0.3 collective-permute-start.5
  24.8 2.4 %collective-permute-done.12.refs_16_ = bf16[512,128]{1,0:T(8,128)(2,1)S(1)} collective-permute-done((bf16[512,128]{1,0:T(8,128)(2,1)S(1)}, bf16[512,128]{1,0:T(8,128)(2,1)S(1)}, u32[]{:S(2)}, u32[]{:S(2)}) %collective-permute-start.12) | collective-permute-done | bytes 131104 | tf_op jit(solution)/shard_map/ppermute | solution.py:159
  27.2 0.4 collective-permute-start.13
  27.6 1.6 %collective-permute-start.6 = (bf16[528,128]{1,0:T(8,128)(2,1)S(1)}, bf16[528,128]{1,0:T(8,128)(2,1)S(1)}, u32[]{:S(2)}, u32[]{:S(2)}) collective-permute-start(bf16[528,128]{1,0:T(8,128)(2,1)S(1)} %collective-permute-done.4.refs_7_), channel_id=1, source_target_pairs={{0,8},{8,16},{16,24},{24,28},{28,20},{20,12},{12,4},{4,0},{1,9},{9... | collective-permute-start | bytes 405512 | tf_op jit(solution)/shard_map/ppermute | solution.py:162
  29.3 0.1 add.73
  29.4 0.7 %copy-done.20 = s32[2]{0:T(128)S(1)} copy-done((s32[2]{0:T(128)S(1)}, s32[2]{0:T(128)}, u32[]{:S(2)}) %copy-start.20) | copy-done | bytes 32
  30.1 0.1 fusion
  30.2 2.0 %collective-permute-done.13.refs_17_ = bf16[512,128]{1,0:T(8,128)(2,1)S(1)} collective-permute-done((bf16[512,128]{1,0:T(8,128)(2,1)S(1)}, bf16[512,128]{1,0:T(8,128)(2,1)S(1)}, u32[]{:S(2)}, u32[]{:S(2)}) %collective-permute-start.13) | collective-permute-done | bytes 131104 | tf_op jit(solution)/shard_map/ppermute | solution.py:163
  32.2 0.4 collective-permute-done.6.refs_9_
  32.6 0.7 %broadcast_in_dim.11.refs_0_ = f32[16,128]{1,0:T(8,128)} broadcast(f32[16]{0:T(128)S(1)} %convert_element_type.12), dimensions={0} | broadcast | bytes 8256 | tf_op jit(solution)/shard_map/broadcast_in_dim | solution.py:142
  33.3 0.7 %broadcast_in_dim.12.refs_1_ = f32[16,128]{1,0:T(8,128)} broadcast(f32[16]{0:T(128)S(1)} %fusion), dimensions={0} | broadcast | bytes 8256 | tf_op jit(solution)/shard_map/broadcast_in_dim | solution.py:143
  34.0 8.8 %shard_map.112 = (bf16[2,128,128]{2,1,0:T(8,128)(2,1)}, bf16[2,128,128]{2,1,0:T(8,128)(2,1)}, bf16[2,128,128]{2,1,0:T(8,128)(2,1)}) custom-call(f32[16,128]{1,0:T(8,128)} %broadcast_in_dim.11.refs_0_, f32[16,128]{1,0:T(8,128)} %broadcast_in_dim.12.refs_1_, bf16[528,128]{1,0:T(8,128)(2,1)} %copy-done.1, bf16[528,128]{1,0:T(8,128)(2,1)} %copy-done.3, ...), custom_call_target="tpu_custom_call" | custom-call | tf_op jit(solution)/shard_map/pallas_call | solution.py:170
  (64 shorter events, 0.5 us)
Async XLA Ops:
  1.7 5.0 %copy-start.17 = (bf16[2,128,128]{2,1,0:T(8,128)(2,1)S(1)}, bf16[2,128,128]{2,1,0:T(8,128)(2,1)}, u32[]{:S(2)}) copy-start(bf16[2,128,128]{2,1,0:T(8,128)(2,1)} %param.12) | copy-start | bytes 196612
  1.7 5.0 %copy-start.18 = (bf16[2,128,128]{2,1,0:T(8,128)(2,1)S(1)}, bf16[2,128,128]{2,1,0:T(8,128)(2,1)}, u32[]{:S(2)}) copy-start(bf16[2,128,128]{2,1,0:T(8,128)(2,1)} %param.9) | copy-start | bytes 196612
  3.6 5.3 %copy-start.1 = (bf16[528,128]{1,0:T(8,128)(2,1)}, bf16[528,128]{1,0:T(8,128)(2,1)S(1)}, u32[]{:S(2)}) copy-start(bf16[528,128]{1,0:T(8,128)(2,1)S(1)} %concatenate.9.refs_2_) | copy-start | bytes 405508
  3.6 9.6 %collective-permute-start = (bf16[528,128]{1,0:T(8,128)(2,1)S(1)}, bf16[528,128]{1,0:T(8,128)(2,1)S(1)}, u32[]{:S(2)}, u32[]{:S(2)}) collective-permute-start(bf16[528,128]{1,0:T(8,128)(2,1)S(1)} %concatenate.9.refs_2_), channel_id=1, source_target_pairs={{0,8},{8,16},{16,24},{24,28},{28,20},{20,12},{12,4},{4,0},{1,9},{9... | collective-permute-start | bytes 405512 | tf_op jit(solution)/shard_map/ppermute | solution.py:158
  6.7 9.8 %copy-start.2 = (bf16[512,128]{1,0:T(8,128)(2,1)}, bf16[512,128]{1,0:T(8,128)(2,1)S(1)}, u32[]{:S(2)}) copy-start(bf16[512,128]{1,0:T(8,128)(2,1)S(1)} %pad_maximum_fusion.refs_10_) | copy-start | bytes 393220
  6.7 6.4 %collective-permute-start.8 = (bf16[512,128]{1,0:T(8,128)(2,1)S(1)}, bf16[512,128]{1,0:T(8,128)(2,1)S(1)}, u32[]{:S(2)}, u32[]{:S(2)}) collective-permute-start(bf16[512,128]{1,0:T(8,128)(2,1)S(1)} %pad_maximum_fusion.refs_10_), channel_id=1, source_target_pairs={{8,0},{16,8},{24,16},{28,24},{20,28},{12,20},{4,12},{0,4},{9,1},{1... | collective-permute-start | bytes 393224 | tf_op jit(solution)/shard_map/ppermute | solution.py:159
  6.8 9.7 %collective-permute-start.7 = (bf16[512,128]{1,0:T(8,128)(2,1)S(1)}, bf16[512,128]{1,0:T(8,128)(2,1)S(1)}, u32[]{:S(2)}, u32[]{:S(2)}) collective-permute-start(bf16[512,128]{1,0:T(8,128)(2,1)S(1)} %pad_maximum_fusion.refs_10_), channel_id=1, source_target_pairs={{0,8},{8,16},{16,24},{24,28},{28,20},{20,12},{12,4},{4,0},{1,9},{9... | collective-permute-start | bytes 393224 | tf_op jit(solution)/shard_map/ppermute | solution.py:159
  8.8 9.3 %collective-permute-start.1 = (bf16[528,128]{1,0:T(8,128)(2,1)S(1)}, bf16[528,128]{1,0:T(8,128)(2,1)S(1)}, u32[]{:S(2)}, u32[]{:S(2)}) collective-permute-start(bf16[528,128]{1,0:T(8,128)(2,1)S(1)} %concatenate.9.refs_2_), channel_id=1, source_target_pairs={{8,0},{16,8},{24,16},{28,24},{20,28},{12,20},{4,12},{0,4},{9,1},{1... | collective-permute-start | bytes 405512 | tf_op jit(solution)/shard_map/ppermute | solution.py:158
  10.1 5.0 %copy-start.21 = (s32[8]{0:T(128)S(1)}, s32[8]{0:T(128)}, u32[]{:S(2)}) copy-start(s32[8]{0:T(128)} %constant.57.clone) | copy-start | bytes 100
  13.1 3.4 %copy-start.10 = (bf16[512,128]{1,0:T(8,128)(2,1)}, bf16[512,128]{1,0:T(8,128)(2,1)S(1)}, u32[]{:S(2)}) copy-start(bf16[512,128]{1,0:T(8,128)(2,1)S(1)} %collective-permute-done.8.refs_12_) | copy-start | bytes 393220
  13.1 5.8 %collective-permute-start.10 = (bf16[512,128]{1,0:T(8,128)(2,1)S(1)}, bf16[512,128]{1,0:T(8,128)(2,1)S(1)}, u32[]{:S(2)}, u32[]{:S(2)}) collective-permute-start(bf16[512,128]{1,0:T(8,128)(2,1)S(1)} %collective-permute-done.8.refs_12_), channel_id=1, source_target_pairs={{8,0},{16,8},{24,16},{28,24},{20,28},{12,20},{4,12},{0,4},{9,1},{1... | collective-permute-start | bytes 393224 | tf_op jit(solution)/shard_map/ppermute | solution.py:159
  13.2 3.3 %copy-start.3 = (bf16[528,128]{1,0:T(8,128)(2,1)}, bf16[528,128]{1,0:T(8,128)(2,1)S(1)}, u32[]{:S(2)}) copy-start(bf16[528,128]{1,0:T(8,128)(2,1)S(1)} %collective-permute-done.refs_3_) | copy-start | bytes 405508
  13.2 5.8 %collective-permute-start.2 = (bf16[528,128]{1,0:T(8,128)(2,1)S(1)}, bf16[528,128]{1,0:T(8,128)(2,1)S(1)}, u32[]{:S(2)}, u32[]{:S(2)}) collective-permute-start(bf16[528,128]{1,0:T(8,128)(2,1)S(1)} %collective-permute-done.refs_3_), channel_id=1, source_target_pairs={{0,8},{8,16},{16,24},{24,28},{28,20},{20,12},{12,4},{4,0},{1,9},{9... | collective-permute-start | bytes 405512 | tf_op jit(solution)/shard_map/ppermute | solution.py:158
  16.5 17.4 %copy-start.11 = (bf16[512,128]{1,0:T(8,128)(2,1)}, bf16[512,128]{1,0:T(8,128)(2,1)S(1)}, u32[]{:S(2)}) copy-start(bf16[512,128]{1,0:T(8,128)(2,1)S(1)} %collective-permute-done.7.refs_11_) | copy-start | bytes 393220
  16.5 6.1 %collective-permute-start.9 = (bf16[512,128]{1,0:T(8,128)(2,1)S(1)}, bf16[512,128]{1,0:T(8,128)(2,1)S(1)}, u32[]{:S(2)}, u32[]{:S(2)}) collective-permute-start(bf16[512,128]{1,0:T(8,128)(2,1)S(1)} %collective-permute-done.7.refs_11_), channel_id=1, source_target_pairs={{0,8},{8,16},{16,24},{24,28},{28,20},{20,12},{12,4},{4,0},{1,9},{9... | collective-permute-start | bytes 393224 | tf_op jit(solution)/shard_map/ppermute | solution.py:159
  18.2 15.8 %copy-start.4 = (bf16[528,128]{1,0:T(8,128)(2,1)}, bf16[528,128]{1,0:T(8,128)(2,1)S(1)}, u32[]{:S(2)}) copy-start(bf16[528,128]{1,0:T(8,128)(2,1)S(1)} %collective-permute-done.1.refs_4_) | copy-start | bytes 405508
  18.2 6.4 %collective-permute-start.3 = (bf16[528,128]{1,0:T(8,128)(2,1)S(1)}, bf16[528,128]{1,0:T(8,128)(2,1)S(1)}, u32[]{:S(2)}, u32[]{:S(2)}) collective-permute-start(bf16[528,128]{1,0:T(8,128)(2,1)S(1)} %collective-permute-done.1.refs_4_), channel_id=1, source_target_pairs={{8,0},{16,8},{24,16},{28,24},{20,28},{12,20},{4,12},{0,4},{9,1},{1... | collective-permute-start | bytes 405512 | tf_op jit(solution)/shard_map/ppermute | solution.py:158
  18.9 15.1 %copy-start.12 = (bf16[512,128]{1,0:T(8,128)(2,1)}, bf16[512,128]{1,0:T(8,128)(2,1)S(1)}, u32[]{:S(2)}) copy-start(bf16[512,128]{1,0:T(8,128)(2,1)S(1)} %collective-permute-done.10.refs_14_) | copy-start | bytes 393220
  18.9 8.3 %collective-permute-start.12 = (bf16[512,128]{1,0:T(8,128)(2,1)S(1)}, bf16[512,128]{1,0:T(8,128)(2,1)S(1)}, u32[]{:S(2)}, u32[]{:S(2)}) collective-permute-start(bf16[512,128]{1,0:T(8,128)(2,1)S(1)} %collective-permute-done.10.refs_14_), channel_id=1, source_target_pairs={{8,0},{16,8},{24,16},{28,24},{20,28},{12,20},{4,12},{0,4},{9,1},{1... | collective-permute-start | bytes 393224 | tf_op jit(solution)/shard_map/ppermute | solution.py:159
  19.0 15.0 %copy-start.5 = (bf16[528,128]{1,0:T(8,128)(2,1)}, bf16[528,128]{1,0:T(8,128)(2,1)S(1)}, u32[]{:S(2)}) copy-start(bf16[528,128]{1,0:T(8,128)(2,1)S(1)} %collective-permute-done.2.refs_5_) | copy-start | bytes 405508
  19.0 8.6 %collective-permute-start.4 = (bf16[528,128]{1,0:T(8,128)(2,1)S(1)}, bf16[528,128]{1,0:T(8,128)(2,1)S(1)}, u32[]{:S(2)}, u32[]{:S(2)}) collective-permute-start(bf16[528,128]{1,0:T(8,128)(2,1)S(1)} %collective-permute-done.2.refs_5_), channel_id=1, source_target_pairs={{0,8},{8,16},{16,24},{24,28},{28,20},{20,12},{12,4},{4,0},{1,9},{9... | collective-permute-start | bytes 405512 | tf_op jit(solution)/shard_map/ppermute | solution.py:158
  22.6 11.3 %copy-start.13 = (bf16[512,128]{1,0:T(8,128)(2,1)}, bf16[512,128]{1,0:T(8,128)(2,1)S(1)}, u32[]{:S(2)}) copy-start(bf16[512,128]{1,0:T(8,128)(2,1)S(1)} %collective-permute-done.9.refs_13_) | copy-start | bytes 393220
  22.6 7.5 %collective-permute-start.11 = (bf16[512,128]{1,0:T(8,128)(2,1)S(1)}, bf16[512,128]{1,0:T(8,128)(2,1)S(1)}, u32[]{:S(2)}, u32[]{:S(2)}) collective-permute-start(bf16[512,128]{1,0:T(8,128)(2,1)S(1)} %collective-permute-done.9.refs_13_), channel_id=1, source_target_pairs={{0,8},{8,16},{16,24},{24,28},{28,20},{20,12},{12,4},{4,0},{1,9},{9... | collective-permute-start | bytes 393224 | tf_op jit(solution)/shard_map/ppermute | solution.py:159
  24.5 9.4 %copy-start.6 = (bf16[528,128]{1,0:T(8,128)(2,1)}, bf16[528,128]{1,0:T(8,128)(2,1)S(1)}, u32[]{:S(2)}) copy-start(bf16[528,128]{1,0:T(8,128)(2,1)S(1)} %collective-permute-done.3.refs_6_) | copy-start | bytes 405508
  24.5 5.6 %collective-permute-start.5 = (bf16[528,128]{1,0:T(8,128)(2,1)S(1)}, bf16[528,128]{1,0:T(8,128)(2,1)S(1)}, u32[]{:S(2)}, u32[]{:S(2)}) collective-permute-start(bf16[528,128]{1,0:T(8,128)(2,1)S(1)} %collective-permute-done.3.refs_6_), channel_id=1, source_target_pairs={{8,0},{16,8},{24,16},{28,24},{20,28},{12,20},{4,12},{0,4},{9,1},{1... | collective-permute-start | bytes 405512 | tf_op jit(solution)/shard_map/ppermute | solution.py:158
  27.2 6.8 %copy-start.14 = (bf16[512,128]{1,0:T(8,128)(2,1)}, bf16[512,128]{1,0:T(8,128)(2,1)S(1)}, u32[]{:S(2)}) copy-start(bf16[512,128]{1,0:T(8,128)(2,1)S(1)} %collective-permute-done.12.refs_16_) | copy-start | bytes 393220
  27.2 5.0 %collective-permute-start.13 = (bf16[512,128]{1,0:T(8,128)(2,1)S(1)}, bf16[512,128]{1,0:T(8,128)(2,1)S(1)}, u32[]{:S(2)}, u32[]{:S(2)}) collective-permute-start(bf16[512,128]{1,0:T(8,128)(2,1)S(1)} %collective-permute-done.12.refs_16_), channel_id=1, source_target_pairs={{8,0},{16,8},{24,16},{28,24},{20,28},{12,20},{4,12},{0,4},{9,1},{1... | collective-permute-start | bytes 393224 | tf_op jit(solution)/shard_map/ppermute | solution.py:163
  27.6 6.4 %copy-start.7 = (bf16[528,128]{1,0:T(8,128)(2,1)}, bf16[528,128]{1,0:T(8,128)(2,1)S(1)}, u32[]{:S(2)}) copy-start(bf16[528,128]{1,0:T(8,128)(2,1)S(1)} %collective-permute-done.4.refs_7_) | copy-start | bytes 405508
  27.6 5.0 %collective-permute-start.6 = (bf16[528,128]{1,0:T(8,128)(2,1)S(1)}, bf16[528,128]{1,0:T(8,128)(2,1)S(1)}, u32[]{:S(2)}, u32[]{:S(2)}) collective-permute-start(bf16[528,128]{1,0:T(8,128)(2,1)S(1)} %collective-permute-done.4.refs_7_), channel_id=1, source_target_pairs={{0,8},{8,16},{16,24},{24,28},{28,20},{20,12},{12,4},{4,0},{1,9},{9... | collective-permute-start | bytes 405512 | tf_op jit(solution)/shard_map/ppermute | solution.py:162
  30.2 3.8 %copy-start.15 = (bf16[512,128]{1,0:T(8,128)(2,1)}, bf16[512,128]{1,0:T(8,128)(2,1)S(1)}, u32[]{:S(2)}) copy-start(bf16[512,128]{1,0:T(8,128)(2,1)S(1)} %collective-permute-done.11.refs_15_) | copy-start | bytes 393220
  30.2 3.8 %copy-start.8 = (bf16[528,128]{1,0:T(8,128)(2,1)}, bf16[528,128]{1,0:T(8,128)(2,1)S(1)}, u32[]{:S(2)}) copy-start(bf16[528,128]{1,0:T(8,128)(2,1)S(1)} %collective-permute-done.5.refs_8_) | copy-start | bytes 405508
  32.2 1.8 %copy-start.16 = (bf16[512,128]{1,0:T(8,128)(2,1)}, bf16[512,128]{1,0:T(8,128)(2,1)S(1)}, u32[]{:S(2)}) copy-start(bf16[512,128]{1,0:T(8,128)(2,1)S(1)} %collective-permute-done.13.refs_17_) | copy-start | bytes 393220
  (5 other events, 4.1 us)

commit v2 on v0

--- a/solution.py
+++ b/solution.py
@@ -1,9 +1,303 @@
+import functools
 import math
 
 import jax
 import jax.numpy as jnp
 from jax import lax
+from jax.experimental import pallas as pl
+from jax.experimental.pallas import tpu as pltpu
 from jax.sharding import PartitionSpec as P
+
+GATHER_BYTES = 8 * 2**20
+LOG2E = math.log2(math.e)
+NEVER = -1e30
+NT = (((1,), (1,)), ((), ()))
+
+
+def ring_order(count):
+    return list(range(0, count, 2)) + list(range(1, count, 2))[::-1]
+
+
+def pack_kernel(sizes, ids_ref, gids_ref, k_ref, v_ref, q_ref, g_ref, a_ref, b_ref, sems):
+    heads, count, rows, width, block_rows, slots, _ = sizes
+    blocks = rows // block_rows
+    copies = []
+    for i, (src, dst, first) in enumerate(
+        ((k_ref, a_ref, 0), (v_ref, a_ref, heads), (q_ref, b_ref, 0), (g_ref, b_ref, heads))
+    ):
+        for h in range(heads):
+            copies.append(
+                pltpu.make_async_copy(
+                    src.at[h], dst.at[pl.ds((first + h) * rows, rows)], sems.at[i * heads + h]
+                )
+            )
+    for c in copies:
+        c.start()
+    head_rows = a_ref.shape[0] - 2 * heads * rows
+    row = lax.broadcasted_iota(jnp.int32, (head_rows, rows), 0)
+    lane = lax.broadcasted_iota(jnp.int32, (head_rows, rows), 1)
+    me = lax.axis_index("seq")
+    block = jnp.zeros_like(lane)
+    for n in range(1, blocks):
+        block = block + jnp.where(lane >= n * block_rows, 1, 0)
+    tile = me * blocks + block
+    for h in range(heads):
+        for j in range(slots):
+            ids = jnp.full_like(lane, ids_ref[h, 0, j])
+            for n in range(1, blocks):
+                ids = jnp.where(block == n, ids_ref[h, n, j], ids)
+            tile = jnp.where(row == h * slots + j, ids, tile)
+    for n in range(gids_ref.shape[0]):
+        tile = jnp.where(row == heads * slots + 1 + n, gids_ref[n], tile)
+    a_ref[2 * heads * rows :] = tile.astype(jnp.float32).astype(jnp.bfloat16)
+    for c in copies:
+        c.wait()
+
+
+class Shards:
+    def __init__(self, sizes, a_refs, b_refs):
+        self.heads, self.count, self.rows, self.width, self.block_rows, self.slots, self.gids = sizes
+        self.blocks = self.rows // self.block_rows
+        self.a, self.b = a_refs, b_refs
+        self.scale = 1.0 / math.sqrt(self.width)
+        self.rate = self.scale * LOG2E
+        self.heads_of = {s: self.head(s) for s in a_refs}
+
+    def part(self, refs, index, group):
+        found = [refs[s][index * self.rows : (index + 1) * self.rows] for s in group]
+        return found[0] if len(found) == 1 else jnp.concatenate(found)
+
+    def k(self, h, group):
+        return self.part(self.a, h, group)
+
+    def v(self, h, group):
+        return self.part(self.a, self.heads + h, group)
+
+    def q(self, h, group):
+        return self.part(self.b, h, group)
+
+    def g(self, h, group):
+        return self.part(self.b, self.heads + h, group)
+
+    def key_ids(self, group):
+        height = len(group) * self.blocks
+        row = lax.broadcasted_iota(jnp.int32, (height, self.rows), 0).astype(jnp.float32)
+        base = self.heads * self.slots
+        nk = jnp.zeros((height, self.rows), jnp.float32)
+        for i, s in enumerate(group):
+            first = self.heads_of[s][base : base + 1, 0:1] - i * self.blocks
+            nk = jnp.where(row >= i * self.blocks, row + first, nk)
+        seen = jnp.zeros((height, self.rows), jnp.float32)
+        for n in range(self.gids):
+            gid = self.heads_of[group[0]][base + 1 + n : base + 2 + n]
+            seen = seen + jnp.where(nk == gid, 1.0, 0.0)
+        return nk, seen
+
+    def head(self, s):
+        return self.a[s][2 * self.heads * self.rows :].astype(jnp.float32)
+
+    def bias(self, keys, group):
+        nk, seen = keys
+        out = []
+        for h in range(self.heads):
+            cols = []
+            for s in group:
+                head = self.heads_of[s]
+                nq = head[self.heads * self.slots :][:1]
+                count = seen + jnp.where(jnp.abs(nk - nq) <= 1.0, 1.0, 0.0)
+                for j in range(self.slots):
+                    r = h * self.slots + j
+                    count = count + jnp.where(nk == head[r : r + 1], 1.0, 0.0)
+                cols.append(jnp.where(count > 0.5, jnp.log2(jnp.maximum(count, 1.0)), NEVER))
+            out.append(cols[0] if len(cols) == 1 else jnp.concatenate(cols, axis=1))
+        return out
+
+    def scores(self, h, keys, queries):
+        return (
+            lax.dot_general(self.k(h, keys), self.q(h, queries), NT, preferred_element_type=jnp.float32),
+            lax.dot_general(self.v(h, keys), self.g(h, queries), NT, preferred_element_type=jnp.float32),
+        )
+
+    def stats(self, scored, bias):
+        s, dp = scored
+        lanes = s.shape[1]
+        steps = self.block_rows // 8
+        top = None
+        for kb in range(bias.shape[0]):
+            x = s[kb * self.block_rows : (kb + 1) * self.block_rows] * self.rate + bias[kb : kb + 1]
+            x = jnp.max(x.reshape(steps, 8, lanes), axis=0)
+            top = x if top is None else jnp.maximum(top, x)
+        top = jnp.maximum(jnp.max(top, axis=0, keepdims=True), 0.5 * NEVER)
+        acc_l = acc_d = None
+        for kb in range(bias.shape[0]):
+            cut = slice(kb * self.block_rows, (kb + 1) * self.block_rows)
+            e = jnp.exp2(s[cut] * self.rate + (bias[kb : kb + 1] - top))
+            d = jnp.sum((e * dp[cut]).reshape(steps, 8, lanes), axis=0)
+            e = jnp.sum(e.reshape(steps, 8, lanes), axis=0)
+            acc_l = e if acc_l is None else acc_l + e
+            acc_d = d if acc_d is None else acc_d + d
+        return top, jnp.sum(acc_l, axis=0, keepdims=True), jnp.sum(acc_d, axis=0, keepdims=True)
+
+
+def merged(parts):
+    if len(parts) == 1:
+        return parts[0]
+    top = functools.reduce(jnp.maximum, [p[0] for p in parts])
+    weights = [jnp.exp2(p[0] - top) for p in parts]
+    return top, sum(p[1] * w for p, w in zip(parts, weights)), sum(p[2] * w for p, w in zip(parts, weights))
+
+
+def rect_stats(sh, keys, queries):
+    ids = sh.key_ids(keys)
+    found = {}
+    pairs = [queries[i : i + 2] for i in range(0, len(queries), 2)]
+    for group in pairs:
+        bias = sh.bias(ids, group)
+        for h in range(sh.heads):
+            got = sh.stats(sh.scores(h, keys, group), bias[h])
+            for i, s in enumerate(group):
+                found[h, s] = tuple(x[:, i * sh.rows : (i + 1) * sh.rows] for x in got)
+    return found
+
+
+def stats_kernel(sizes, slots_in, before, rects, *refs):
+    heads = sizes[0]
+    n = len(slots_in)
+    a_refs = dict(zip(slots_in, refs[:n]))
+    b_refs = dict(zip(slots_in, refs[n : 2 * n]))
+    rest = refs[2 * n :]
+    old = rest[0] if before else None
+    out = rest[-1]
+    sh = Shards(sizes, a_refs, b_refs)
+    parts = {}
+    for keys, queries in rects:
+        for where, got in rect_stats(sh, keys, queries).items():
+            parts.setdefault(where, []).append(got)
+    for (h, s), found in parts.items():
+        if s in before:
+            found.append(tuple(old[s, 3 * h + i : 3 * h + i + 1] for i in range(3)))
+        for i, x in enumerate(merged(found)):
+            out[s, 3 * h + i : 3 * h + i + 1] = x
+
+
+def final_kernel(sizes, before, rects, *refs):
+    heads, count = sizes[:2]
+    a_refs = dict(enumerate(refs[:count]))
+    b_refs = dict(enumerate(refs[count : 2 * count]))
+    old, dq_ref, dk_ref, dv_ref = refs[2 * count :]
+    sh = Shards(sizes, a_refs, b_refs)
+    every = list(range(count))
+    parts = {}
+    for keys, queries in rects:
+        for where, got in rect_stats(sh, keys, queries).items():
+            parts.setdefault(where, []).append(got)
+    shift, dot_row = {}, {}
+    for (h, s), found in parts.items():
+        if s in before:
+            found.append(tuple(old[s, 3 * h + i : 3 * h + i + 1] for i in range(3)))
+        top, total, weighted = merged(found)
+        shift[h, s] = top + jnp.log2(total)
+        dot_row[h, s] = weighted / total
+    own_ids, all_ids = sh.key_ids([0]), sh.key_ids(every)
+    row_bias = sh.bias(all_ids, [0])
+    for h in range(heads):
+        dk = dv = None
+        for first in range(0, count, 2):
+            group = every[first : first + 2]
+            bias = sh.bias(own_ids, group)[h]
+            s, dp = sh.scores(h, [0], group)
+            bias = bias - jnp.concatenate([shift[h, i] for i in group], axis=1)
+            dots = jnp.concatenate([dot_row[h, i] for i in group], axis=1)
+            p_low, ds_low = weights(sh, s, dp, bias, dots)
+            v_term = jnp.dot(p_low, sh.g(h, group), preferred_element_type=jnp.float32)
+            k_term = jnp.dot(ds_low, sh.q(h, group), preferred_element_type=jnp.float32)
+            dv = v_term if dv is None else dv + v_term
+            dk = k_term if dk is None else dk + k_term
+        dk_ref[h] = (dk * sh.scale).astype(dk_ref.dtype)
+        dv_ref[h] = dv.astype(dv_ref.dtype)
+        s, dp = sh.scores(h, every, [0])
+        _, ds_low = weights(sh, s, dp, row_bias[h] - shift[h, 0], dot_row[h, 0])
+        dq = lax.dot_general(
+            ds_low, sh.k(h, every), (((0,), (0,)), ((), ())), preferred_element_type=jnp.float32
+        )
+        dq_ref[h] = (dq * sh.scale).astype(dq_ref.dtype)
+
+
+def weights(sh, s, dp, bias, dots):
+    p_low, ds_low = [], []
+    for kb in range(bias.shape[0]):
+        cut = slice(kb * sh.block_rows, (kb + 1) * sh.block_rows)
+        p = jnp.exp2(s[cut] * sh.rate + bias[kb : kb + 1])
+        p_low.append(p.astype(jnp.bfloat16))
+        ds_low.append((p * (dp[cut] - dots)).astype(jnp.bfloat16))
+    return jnp.concatenate(p_low), jnp.concatenate(ds_low)
+
+
+def near(arrays):
+    return [pltpu.with_memory_space_constraint(x, pltpu.VMEM) for x in arrays]
+
+
+def gathered(queries, keys, values, grad_out, rand_ids, global_ids):
+    heads, rows, width = queries.shape
+    blocks, slots = rand_ids.shape[1:]
+    count = lax.axis_size("seq")
+    ring = ring_order(count)
+    forward = [(ring[i], ring[(i + 1) % count]) for i in range(count)]
+    backward = [(b, a) for a, b in forward]
+    half = count // 2
+    sizes = (heads, count, rows, width, rows // blocks, slots, global_ids.shape[0])
+    head_rows = -(-(heads * slots + 1 + global_ids.shape[0]) // 16) * 16
+    vmem = pl.BlockSpec(memory_space=pltpu.VMEM)
+    smem = pl.BlockSpec(memory_space=pltpu.SMEM)
+    anyspace = pl.BlockSpec(memory_space=pl.ANY)
+    a, b = pl.pallas_call(
+        functools.partial(pack_kernel, sizes),
+        out_shape=(
+            pltpu.VMEM((2 * heads * rows + head_rows, width), queries.dtype),
+            pltpu.VMEM((2 * heads * rows, width), queries.dtype),
+        ),
+        in_specs=[smem, smem] + [anyspace] * 4,
+        out_specs=(vmem, vmem),
+        scratch_shapes=[pltpu.SemaphoreType.DMA((4 * heads,))],
+    )(rand_ids, global_ids, keys, values, queries, grad_out)
+
+    a_all, b_all = [a], [b]
+    af = ab = a
+    bf = bb = b
+    stat = None
+    stat_shape = pltpu.VMEM((count, 8, rows), jnp.float32)
+    for d in range(1, half):
+        af, ab = lax.ppermute(af, "seq", forward), lax.ppermute(ab, "seq", backward)
+        bf, bb = lax.ppermute(bf, "seq", forward), lax.ppermute(bb, "seq", backward)
+        a_all += [af, ab]
+        b_all += [bf, bb]
+        if d < half - 2:
+            continue
+        now = list(range(2 * d + 1))
+        if stat is None:
+            before, rects = [], [(now, now)]
+        else:
+            before, new = now[:-2], now[-2:]
+            rects = [(new, before), (now, new)]
+        stat = pl.pallas_call(
+            functools.partial(stats_kernel, sizes, now, before, rects),
+            out_shape=stat_shape,
+            in_specs=[vmem] * (2 * len(now) + bool(before)),
+            out_specs=vmem,
+            cost_estimate=pl.CostEstimate(flops=10**9, bytes_accessed=10**6, transcendentals=10**6),
+        )(*near(a_all), *near(b_all), *near([stat] if before else []))
+    a_all.append(lax.ppermute(af, "seq", forward))
+    b_all.append(lax.ppermute(bb, "seq", backward))
+    every = list(range(count))
+    before = every[:-1]
+    rects = [(every[-1:], before), (every, every[-1:])]
+    out = jax.ShapeDtypeStruct(queries.shape, queries.dtype)
+    return pl.pallas_call(
+        functools.partial(final_kernel, sizes, before, rects),
+        out_shape=(out, out, out),
+        in_specs=[vmem] * (2 * count + 1),
+        out_specs=(vmem, vmem, vmem),
+    )(*near(a_all), *near(b_all), *near([stat]))
 
 
 def with_halo(value, sides, width):
@@ -29,7 +323,7 @@
     return list(range(section_count))
 
 
-def on_device(queries, keys, values, grad_out, rand_ids, global_ids):
+def routed(queries, keys, values, grad_out, rand_ids, global_ids):
     head_count, row_count, head_width = queries.shape
     block_count = rand_ids.shape[1]
     slot_count = rand_ids.shape[2]
@@ -174,6 +468,15 @@
     return (grad_queries, grad_keys, grad_values)
 
 
+def on_device(queries, keys, values, grad_out, rand_ids, global_ids):
+    count = lax.axis_size("seq")
+    rows, width = queries.shape[1:]
+    gathered_bytes = 4 * count * queries.size * queries.dtype.itemsize
+    if gathered_bytes <= GATHER_BYTES and count % 2 == 0 and rows == width:
+        return gathered(queries, keys, values, grad_out, rand_ids, global_ids)
+    return routed(queries, keys, values, grad_out, rand_ids, global_ids)
+
+
 def solution(mesh):
     in_specs = (
         P("head", "seq", None),

time: 175 us -> 32.9 us (0.19)
  waiting for transfers between devices: 71.9 us -> 7.93 us
  blocking collectives: 38.6 us -> 0 us
  between operations: 14.6 us -> 0.69 us
  starting transfers between devices: 27.4 us -> 15.7 us
  local copies, waits for them, and re-layouts: 10.8 us -> 0 us
  Pallas kernels: 0 us -> 8.31 us
  matrix products: 7.31 us -> 0 us
  other arithmetic: 3.48 us -> 0 us
    psum x1 -> x0, waiting for transfers between devices: 43.2 us -> none  [on_device(): global_total = lax.psum(global_part, 'seq')]
    psum x1 -> x0, blocking collectives: 38.6 us -> none  [on_device(): global_sum = lax.psum(picked * owned[None, None, :, None, None], 'seq')]
    ppermute x20 -> x14, waiting for transfers between devices: 28.7 us -> 7.93 us  [the longest x3 5.02 us: gathered(): lax.ppermute(ab, 'seq', backward)]
    ppermute x20 -> x14, starting transfers between devices: 27.4 us -> 15.7 us  [the longest x3 7.16 us: gathered(): lax.ppermute(af, 'seq', forward)]
    pallas_call x0 -> x4, Pallas kernels: none -> 8.31 us  [the longest x1 3.62 us: gathered(): pl.pallas_call(functools.partial(final_kernel, sizes, before, rects), out...]
    dot_general x9 -> x0, matrix products: 7.31 us -> none  [the longest x1 1.94 us: on_device(): jnp.einsum('hqjl,chqjbd->jchlbd', local_float, random_part, precision=lax...]
    slice x12 -> x0, local copies, waits for them, and re-layouts: 3.75 us -> none  [the longest x1 1.24 us: on_device(): all_keys[0]]
    scatter-add x2 -> x0, local copies, waits for them, and re-layouts: 2.83 us -> none  [the longest x1 2.62 us: on_device(): own_grads.at[:, :, block_count - 1]]
  transfers between devices with their start and end apart: 21 -> 14, of which waited for: 14 -> 4; matrix products, arithmetic and copies ran while one was open for 6% -> 0% of each run, Pallas kernels for 0% -> 9%
where the time goes in v2:
time: 32.9 us; the launch traced here: 32.7 us
  starting transfers between devices  15.7 us (48%)
  Pallas kernels  8.31 us (25%)
  waiting for transfers between devices  7.93 us (24%)
  between operations  0.69 us (2%)
    ppermute x3, starting transfers between devices, gathered(): lax.ppermute(af, 'seq', forward)  7.16 us
    ppermute x3, waiting for transfers between devices, gathered(): lax.ppermute(ab, 'seq', backward)  5.02 us
    ppermute x3, starting transfers between devices, gathered(): lax.ppermute(bf, 'seq', forward)  3.99 us
    pallas_call x1, Pallas kernels, gathered(): pl.pallas_call(functools.partial(final_kernel, sizes, before, rects), out...  3.62 us
    pallas_call x2, Pallas kernels, gathered(): pl.pallas_call(functools.partial(stats_kernel, sizes, now, before, rects)...  3.05 us
    ppermute x3, starting transfers between devices, gathered(): lax.ppermute(ab, 'seq', backward)  2.1 us
    ppermute x1, starting transfers between devices, gathered(): a_all.append(lax.ppermute(af, 'seq', forward))  1.95 us
    ppermute x3, waiting for transfers between devices, gathered(): lax.ppermute(af, 'seq', forward)  1.93 us
  transfers between devices with their start and end apart: 14, of which 4 were waited for; matrix products, arithmetic and copies ran while one was open for 0% of the time, Pallas kernels for 9%

profile of v2, /device:TPU:0, one launch (start us, length us, event | category | flops | bytes accessed | tf_op | source)
XLA Modules:
  0.0 32.7 jit_solution(7025275016824373804)
XLA Ops:
  0.6 1.6 %shard_map.85 = (bf16[528,128]{1,0:T(8,128)(2,1)S(1)}, bf16[512,128]{1,0:T(8,128)(2,1)S(1)}) custom-call(s32[2,2,3]{2,1,0:T(2,128)} %ids_ref.1, s32[2]{0:T(128)} %gids_ref.1, bf16[2,128,128]{2,1,0:T(8,128)(2,1)} %k_ref.1, bf16[2,128,128]{2,1,0:T(8,128)(2,1)} %v_ref.1, bf16[2,128,128]{2,1,0:T(8,128)(2,1)} %q_ref.1, bf16[2,128,128]{2,1,0:T(8,128)(2,1)} %g_ref.1), custom_call_target="tpu_custom_call" | custom-call | tf_op jit(solution)/shard_map/pallas_call | solution.py:253
  2.3 3.1 %collective-permute-start = (bf16[528,128]{1,0:T(8,128)(2,1)S(1)}, bf16[528,128]{1,0:T(8,128)(2,1)S(1)}, u32[]{:S(2)}, u32[]{:S(2)}) collective-permute-start(bf16[528,128]{1,0:T(8,128)(2,1)S(1)} %get-tuple-element.5.refs_0_), channel_id=1, source_target_pairs={{0,8},{8,16},{16,24},{24,28},{28,20},{20,12},{12,4},{4,0},{1,9},{9... | collective-permute-start | bytes 405512 | tf_op jit(solution)/shard_map/ppermute | solution.py:270
  5.4 0.0 collective-permute-start.8
  5.4 2.0 %collective-permute-start.1 = (bf16[528,128]{1,0:T(8,128)(2,1)S(1)}, bf16[528,128]{1,0:T(8,128)(2,1)S(1)}, u32[]{:S(2)}, u32[]{:S(2)}) collective-permute-start(bf16[528,128]{1,0:T(8,128)(2,1)S(1)} %get-tuple-element.5.refs_0_), channel_id=1, source_target_pairs={{8,0},{16,8},{24,16},{28,24},{20,28},{12,20},{4,12},{0,4},{9,1},{1... | collective-permute-start | bytes 405512 | tf_op jit(solution)/shard_map/ppermute | solution.py:270
  7.4 0.1 collective-permute-start.7
  7.4 1.9 %collective-permute-done.refs_1_ = bf16[528,128]{1,0:T(8,128)(2,1)S(1)} collective-permute-done((bf16[528,128]{1,0:T(8,128)(2,1)S(1)}, bf16[528,128]{1,0:T(8,128)(2,1)S(1)}, u32[]{:S(2)}, u32[]{:S(2)}) %collective-permute-start) | collective-permute-done | bytes 135200 | tf_op jit(solution)/shard_map/ppermute | solution.py:270
  9.4 2.5 %collective-permute-start.2 = (bf16[528,128]{1,0:T(8,128)(2,1)S(1)}, bf16[528,128]{1,0:T(8,128)(2,1)S(1)}, u32[]{:S(2)}, u32[]{:S(2)}) collective-permute-start(bf16[528,128]{1,0:T(8,128)(2,1)S(1)} %collective-permute-done.refs_1_), channel_id=1, source_target_pairs={{0,8},{8,16},{16,24},{24,28},{28,20},{20,12},{12,4},{4,0},{1,9},{9... | collective-permute-start | bytes 405512 | tf_op jit(solution)/shard_map/ppermute | solution.py:270
  11.8 0.0 collective-permute-done.8.refs_7_.refs_9_.refs_10_
  11.8 0.0 collective-permute-start.10
  11.8 2.6 %collective-permute-done.1.refs_2_ = bf16[528,128]{1,0:T(8,128)(2,1)S(1)} collective-permute-done((bf16[528,128]{1,0:T(8,128)(2,1)S(1)}, bf16[528,128]{1,0:T(8,128)(2,1)S(1)}, u32[]{:S(2)}, u32[]{:S(2)}) %collective-permute-start.1) | collective-permute-done | bytes 135200 | tf_op jit(solution)/shard_map/ppermute | solution.py:270
  14.5 0.1 collective-permute-start.3
  14.5 0.0 collective-permute-done.7.refs_6_.refs_8_.refs_9_
  14.5 2.0 %collective-permute-start.9 = (bf16[512,128]{1,0:T(8,128)(2,1)S(1)}, bf16[512,128]{1,0:T(8,128)(2,1)S(1)}, u32[]{:S(2)}, u32[]{:S(2)}) collective-permute-start(bf16[512,128]{1,0:T(8,128)(2,1)S(1)} %collective-permute-done.7.refs_6_.refs_8_.refs_9_), channel_id=1, source_target_pairs={{0,8},{8,16},{16,24},{24,28},{28,20},{20,12},{12,4},{4,0},{1,9},{9... | collective-permute-start | bytes 393224 | tf_op jit(solution)/shard_map/ppermute | solution.py:271
  16.5 0.0 collective-permute-done.2.refs_3_
  16.5 1.6 %collective-permute-start.4 = (bf16[528,128]{1,0:T(8,128)(2,1)S(1)}, bf16[528,128]{1,0:T(8,128)(2,1)S(1)}, u32[]{:S(2)}, u32[]{:S(2)}) collective-permute-start(bf16[528,128]{1,0:T(8,128)(2,1)S(1)} %collective-permute-done.2.refs_3_), channel_id=1, source_target_pairs={{0,8},{8,16},{16,24},{24,28},{28,20},{20,12},{12,4},{4,0},{1,9},{9... | collective-permute-start | bytes 405512 | tf_op jit(solution)/shard_map/ppermute | solution.py:270
  18.1 0.0 collective-permute-done.10.refs_9_.refs_11_.refs_12_
  18.1 0.4 %collective-permute-start.12 = (bf16[512,128]{1,0:T(8,128)(2,1)S(1)}, bf16[512,128]{1,0:T(8,128)(2,1)S(1)}, u32[]{:S(2)}, u32[]{:S(2)}) collective-permute-start(bf16[512,128]{1,0:T(8,128)(2,1)S(1)} %collective-permute-done.10.refs_9_.refs_11_.refs_12_), channel_id=1, source_target_pairs={{8,0},{16,8},{24,16},{28,24},{20,28},{12,20},{4,12},{0,4},{9,1},{1... | collective-permute-start | bytes 393224 | tf_op jit(solution)/shard_map/ppermute | solution.py:271
  18.5 2.4 %collective-permute-done.3.refs_4_ = bf16[528,128]{1,0:T(8,128)(2,1)S(1)} collective-permute-done((bf16[528,128]{1,0:T(8,128)(2,1)S(1)}, bf16[528,128]{1,0:T(8,128)(2,1)S(1)}, u32[]{:S(2)}, u32[]{:S(2)}) %collective-permute-start.3) | collective-permute-done | bytes 135200 | tf_op jit(solution)/shard_map/ppermute | solution.py:270
  20.9 0.1 collective-permute-start.5
  21.0 0.0 collective-permute-done.9.refs_8_.refs_10_.refs_11_
  21.0 2.0 %collective-permute-start.11 = (bf16[512,128]{1,0:T(8,128)(2,1)S(1)}, bf16[512,128]{1,0:T(8,128)(2,1)S(1)}, u32[]{:S(2)}, u32[]{:S(2)}) collective-permute-start(bf16[512,128]{1,0:T(8,128)(2,1)S(1)} %collective-permute-done.9.refs_8_.refs_10_.refs_11_), channel_id=1, source_target_pairs={{0,8},{8,16},{16,24},{24,28},{28,20},{20,12},{12,4},{4,0},{1,9},{9... | collective-permute-start | bytes 393224 | tf_op jit(solution)/shard_map/ppermute | solution.py:271
  23.0 1.0 %collective-permute-done.12.refs_13_.refs_14_ = bf16[512,128]{1,0:T(8,128)(2,1)S(1)} collective-permute-done((bf16[512,128]{1,0:T(8,128)(2,1)S(1)}, bf16[512,128]{1,0:T(8,128)(2,1)S(1)}, u32[]{:S(2)}, u32[]{:S(2)}) %collective-permute-start.12) | collective-permute-done | bytes 131104 | tf_op jit(solution)/shard_map/ppermute | solution.py:271
  23.9 0.1 collective-permute-start.13
  24.0 0.0 collective-permute-done.4.refs_5_
  24.0 2.0 %collective-permute-start.6 = (bf16[528,128]{1,0:T(8,128)(2,1)S(1)}, bf16[528,128]{1,0:T(8,128)(2,1)S(1)}, u32[]{:S(2)}, u32[]{:S(2)}) collective-permute-start(bf16[528,128]{1,0:T(8,128)(2,1)S(1)} %collective-permute-done.4.refs_5_), channel_id=1, source_target_pairs={{0,8},{8,16},{16,24},{24,28},{28,20},{20,12},{12,4},{4,0},{1,9},{9... | collective-permute-start | bytes 405512 | tf_op jit(solution)/shard_map/ppermute | solution.py:289
  26.0 1.5 %shard_map.86.refs_14_ = f32[8,8,128]{2,1,0:T(8,128)S(1)} custom-call(bf16[528,128]{1,0:T(8,128)(2,1)S(1)} %get-tuple-element.5.refs_0_, bf16[528,128]{1,0:T(8,128)(2,1)S(1)} %collective-permute-done.refs_1_, bf16[528,128]{1,0:T(8,128)(2,1)S(1)} %collective-permute-done.1.refs_2_, bf16[528,128]{1,0:T(8,128)(2,1)S(1)} %collective-permute-done.2.refs_3_, ...), custom_call_target="tpu_custom_call" | custom-call | flops 1000000000 | bytes 1000000 | tf_op jit(solution)/shard_map/pallas_call | solution.py:282
  27.5 0.0 collective-permute-done.11.refs_12_.refs_13_
  27.5 0.0 collective-permute-done.5.refs_6_
  27.5 1.5 %shard_map.87.refs_16_ = f32[8,8,128]{2,1,0:T(8,128)S(1)} custom-call(bf16[528,128]{1,0:T(8,128)(2,1)S(1)} %get-tuple-element.5.refs_0_, bf16[528,128]{1,0:T(8,128)(2,1)S(1)} %collective-permute-done.refs_1_, bf16[528,128]{1,0:T(8,128)(2,1)S(1)} %collective-permute-done.1.refs_2_, bf16[528,128]{1,0:T(8,128)(2,1)S(1)} %collective-permute-done.2.refs_3_, ...), custom_call_target="tpu_custom_call" | custom-call | flops 1000000000 | bytes 1000000 | tf_op jit(solution)/shard_map/pallas_call | solution.py:282
  29.0 0.0 collective-permute-done.13.refs_15_
  29.1 0.0 collective-permute-done.6.refs_7_
  29.1 3.6 %shard_map.88 = (bf16[2,128,128]{2,1,0:T(8,128)(2,1)}, bf16[2,128,128]{2,1,0:T(8,128)(2,1)}, bf16[2,128,128]{2,1,0:T(8,128)(2,1)}) custom-call(bf16[528,128]{1,0:T(8,128)(2,1)S(1)} %get-tuple-element.5.refs_0_, bf16[528,128]{1,0:T(8,128)(2,1)S(1)} %collective-permute-done.refs_1_, bf16[528,128]{1,0:T(8,128)(2,1)S(1)} %collective-permute-done.1.refs_2_, ...), custom_call_target="tpu_custom_call" | custom-call | tf_op jit(solution)/shard_map/pallas_call | solution.py:295
Async XLA Ops:
  2.3 7.1 %collective-permute-start = (bf16[528,128]{1,0:T(8,128)(2,1)S(1)}, bf16[528,128]{1,0:T(8,128)(2,1)S(1)}, u32[]{:S(2)}, u32[]{:S(2)}) collective-permute-start(bf16[528,128]{1,0:T(8,128)(2,1)S(1)} %get-tuple-element.5.refs_0_), channel_id=1, source_target_pairs={{0,8},{8,16},{16,24},{24,28},{28,20},{20,12},{12,4},{4,0},{1,9},{9... | collective-permute-start | bytes 405512 | tf_op jit(solution)/shard_map/ppermute | solution.py:270
  5.4 6.5 %collective-permute-start.8 = (bf16[512,128]{1,0:T(8,128)(2,1)S(1)}, bf16[512,128]{1,0:T(8,128)(2,1)S(1)}, u32[]{:S(2)}, u32[]{:S(2)}) collective-permute-start(bf16[512,128]{1,0:T(8,128)(2,1)S(1)} %get-tuple-element.6.refs_5_.refs_7_.refs_8_), channel_id=1, source_target_pairs={{8,0},{16,8},{24,16},{28,24},{20,28},{12,20},{4,12},{0,4},{9,1},{1... | collective-permute-start | bytes 393224 | tf_op jit(solution)/shard_map/ppermute | solution.py:271
  5.4 9.1 %collective-permute-start.1 = (bf16[528,128]{1,0:T(8,128)(2,1)S(1)}, bf16[528,128]{1,0:T(8,128)(2,1)S(1)}, u32[]{:S(2)}, u32[]{:S(2)}) collective-permute-start(bf16[528,128]{1,0:T(8,128)(2,1)S(1)} %get-tuple-element.5.refs_0_), channel_id=1, source_target_pairs={{8,0},{16,8},{24,16},{28,24},{20,28},{12,20},{4,12},{0,4},{9,1},{1... | collective-permute-start | bytes 405512 | tf_op jit(solution)/shard_map/ppermute | solution.py:270
  7.4 7.2 %collective-permute-start.7 = (bf16[512,128]{1,0:T(8,128)(2,1)S(1)}, bf16[512,128]{1,0:T(8,128)(2,1)S(1)}, u32[]{:S(2)}, u32[]{:S(2)}) collective-permute-start(bf16[512,128]{1,0:T(8,128)(2,1)S(1)} %get-tuple-element.6.refs_5_.refs_7_.refs_8_), channel_id=1, source_target_pairs={{0,8},{8,16},{16,24},{24,28},{28,20},{20,12},{12,4},{4,0},{1,9},{9... | collective-permute-start | bytes 393224 | tf_op jit(solution)/shard_map/ppermute | solution.py:271
  9.4 7.1 %collective-permute-start.2 = (bf16[528,128]{1,0:T(8,128)(2,1)S(1)}, bf16[528,128]{1,0:T(8,128)(2,1)S(1)}, u32[]{:S(2)}, u32[]{:S(2)}) collective-permute-start(bf16[528,128]{1,0:T(8,128)(2,1)S(1)} %collective-permute-done.refs_1_), channel_id=1, source_target_pairs={{0,8},{8,16},{16,24},{24,28},{28,20},{20,12},{12,4},{4,0},{1,9},{9... | collective-permute-start | bytes 405512 | tf_op jit(solution)/shard_map/ppermute | solution.py:270
  11.8 6.2 %collective-permute-start.10 = (bf16[512,128]{1,0:T(8,128)(2,1)S(1)}, bf16[512,128]{1,0:T(8,128)(2,1)S(1)}, u32[]{:S(2)}, u32[]{:S(2)}) collective-permute-start(bf16[512,128]{1,0:T(8,128)(2,1)S(1)} %collective-permute-done.8.refs_7_.refs_9_.refs_10_), channel_id=1, source_target_pairs={{8,0},{16,8},{24,16},{28,24},{20,28},{12,20},{4,12},{0,4},{9,1},{1... | collective-permute-start | bytes 393224 | tf_op jit(solution)/shard_map/ppermute | solution.py:271
  14.5 6.5 %collective-permute-start.3 = (bf16[528,128]{1,0:T(8,128)(2,1)S(1)}, bf16[528,128]{1,0:T(8,128)(2,1)S(1)}, u32[]{:S(2)}, u32[]{:S(2)}) collective-permute-start(bf16[528,128]{1,0:T(8,128)(2,1)S(1)} %collective-permute-done.1.refs_2_), channel_id=1, source_target_pairs={{8,0},{16,8},{24,16},{28,24},{20,28},{12,20},{4,12},{0,4},{9,1},{1... | collective-permute-start | bytes 405512 | tf_op jit(solution)/shard_map/ppermute | solution.py:270
  14.5 6.5 %collective-permute-start.9 = (bf16[512,128]{1,0:T(8,128)(2,1)S(1)}, bf16[512,128]{1,0:T(8,128)(2,1)S(1)}, u32[]{:S(2)}, u32[]{:S(2)}) collective-permute-start(bf16[512,128]{1,0:T(8,128)(2,1)S(1)} %collective-permute-done.7.refs_6_.refs_8_.refs_9_), channel_id=1, source_target_pairs={{0,8},{8,16},{16,24},{24,28},{28,20},{20,12},{12,4},{4,0},{1,9},{9... | collective-permute-start | bytes 393224 | tf_op jit(solution)/shard_map/ppermute | solution.py:271
  16.5 7.5 %collective-permute-start.4 = (bf16[528,128]{1,0:T(8,128)(2,1)S(1)}, bf16[528,128]{1,0:T(8,128)(2,1)S(1)}, u32[]{:S(2)}, u32[]{:S(2)}) collective-permute-start(bf16[528,128]{1,0:T(8,128)(2,1)S(1)} %collective-permute-done.2.refs_3_), channel_id=1, source_target_pairs={{0,8},{8,16},{16,24},{24,28},{28,20},{20,12},{12,4},{4,0},{1,9},{9... | collective-permute-start | bytes 405512 | tf_op jit(solution)/shard_map/ppermute | solution.py:270
  18.1 5.8 %collective-permute-start.12 = (bf16[512,128]{1,0:T(8,128)(2,1)S(1)}, bf16[512,128]{1,0:T(8,128)(2,1)S(1)}, u32[]{:S(2)}, u32[]{:S(2)}) collective-permute-start(bf16[512,128]{1,0:T(8,128)(2,1)S(1)} %collective-permute-done.10.refs_9_.refs_11_.refs_12_), channel_id=1, source_target_pairs={{8,0},{16,8},{24,16},{28,24},{20,28},{12,20},{4,12},{0,4},{9,1},{1... | collective-permute-start | bytes 393224 | tf_op jit(solution)/shard_map/ppermute | solution.py:271
  20.9 6.6 %collective-permute-start.5 = (bf16[528,128]{1,0:T(8,128)(2,1)S(1)}, bf16[528,128]{1,0:T(8,128)(2,1)S(1)}, u32[]{:S(2)}, u32[]{:S(2)}) collective-permute-start(bf16[528,128]{1,0:T(8,128)(2,1)S(1)} %collective-permute-done.3.refs_4_), channel_id=1, source_target_pairs={{8,0},{16,8},{24,16},{28,24},{20,28},{12,20},{4,12},{0,4},{9,1},{1... | collective-permute-start | bytes 405512 | tf_op jit(solution)/shard_map/ppermute | solution.py:270
  21.0 6.5 %collective-permute-start.11 = (bf16[512,128]{1,0:T(8,128)(2,1)S(1)}, bf16[512,128]{1,0:T(8,128)(2,1)S(1)}, u32[]{:S(2)}, u32[]{:S(2)}) collective-permute-start(bf16[512,128]{1,0:T(8,128)(2,1)S(1)} %collective-permute-done.9.refs_8_.refs_10_.refs_11_), channel_id=1, source_target_pairs={{0,8},{8,16},{16,24},{24,28},{28,20},{20,12},{12,4},{4,0},{1,9},{9... | collective-permute-start | bytes 393224 | tf_op jit(solution)/shard_map/ppermute | solution.py:271
  23.9 5.1 %collective-permute-start.13 = (bf16[512,128]{1,0:T(8,128)(2,1)S(1)}, bf16[512,128]{1,0:T(8,128)(2,1)S(1)}, u32[]{:S(2)}, u32[]{:S(2)}) collective-permute-start(bf16[512,128]{1,0:T(8,128)(2,1)S(1)} %collective-permute-done.12.refs_13_.refs_14_), channel_id=1, source_target_pairs={{8,0},{16,8},{24,16},{28,24},{20,28},{12,20},{4,12},{0,4},{9,1},{1... | collective-permute-start | bytes 393224 | tf_op jit(solution)/shard_map/ppermute | solution.py:290
  24.0 5.1 %collective-permute-start.6 = (bf16[528,128]{1,0:T(8,128)(2,1)S(1)}, bf16[528,128]{1,0:T(8,128)(2,1)S(1)}, u32[]{:S(2)}, u32[]{:S(2)}) collective-permute-start(bf16[528,128]{1,0:T(8,128)(2,1)S(1)} %collective-permute-done.4.refs_5_), channel_id=1, source_target_pairs={{0,8},{8,16},{16,24},{24,28},{28,20},{20,12},{12,4},{4,0},{1,9},{9... | collective-permute-start | bytes 405512 | tf_op jit(solution)/shard_map/ppermute | solution.py:289

commit v3 on v2

--- a/solution.py
+++ b/solution.py
@@ -9,6 +9,7 @@
 from jax.sharding import PartitionSpec as P
 
 GATHER_BYTES = 8 * 2**20
+KERNEL_VMEM = 16 * 2**20
 LOG2E = math.log2(math.e)
 NEVER = -1e30
 NT = (((1,), (1,)), ((), ()))
@@ -18,9 +19,13 @@
     return list(range(0, count, 2)) + list(range(1, count, 2))[::-1]
 
 
-def pack_kernel(sizes, ids_ref, gids_ref, k_ref, v_ref, q_ref, g_ref, a_ref, b_ref, sems):
+def pack_kernel(sizes, ids_hbm, gids_hbm, k_ref, v_ref, q_ref, g_ref, a_ref, b_ref, ids_ref, gids_ref, sems):
     heads, count, rows, width, block_rows, slots, _ = sizes
     blocks = rows // block_rows
+    small = [
+        pltpu.make_async_copy(ids_hbm, ids_ref, sems.at[0]),
+        pltpu.make_async_copy(gids_hbm, gids_ref, sems.at[1]),
+    ]
     copies = []
     for i, (src, dst, first) in enumerate(
         ((k_ref, a_ref, 0), (v_ref, a_ref, heads), (q_ref, b_ref, 0), (g_ref, b_ref, heads))
@@ -28,10 +33,10 @@
         for h in range(heads):
             copies.append(
                 pltpu.make_async_copy(
-                    src.at[h], dst.at[pl.ds((first + h) * rows, rows)], sems.at[i * heads + h]
+                    src.at[h], dst.at[pl.ds((first + h) * rows, rows)], sems.at[2 + i * heads + h]
                 )
             )
-    for c in copies:
+    for c in small + copies:
         c.start()
     head_rows = a_ref.shape[0] - 2 * heads * rows
     row = lax.broadcasted_iota(jnp.int32, (head_rows, rows), 0)
@@ -41,6 +46,8 @@
     for n in range(1, blocks):
         block = block + jnp.where(lane >= n * block_rows, 1, 0)
     tile = me * blocks + block
+    for c in small:
+        c.wait()
     for h in range(heads):
         for j in range(slots):
             ids = jnp.full_like(lane, ids_ref[h, 0, j])
@@ -118,7 +125,7 @@
             lax.dot_general(self.v(h, keys), self.g(h, queries), NT, preferred_element_type=jnp.float32),
         )
 
-    def stats(self, scored, bias):
+    def stats(self, scored, bias, keep):
         s, dp = scored
         lanes = s.shape[1]
         steps = self.block_rows // 8
@@ -132,6 +139,7 @@
         for kb in range(bias.shape[0]):
             cut = slice(kb * self.block_rows, (kb + 1) * self.block_rows)
             e = jnp.exp2(s[cut] * self.rate + (bias[kb : kb + 1] - top))
+            keep(kb, cut, e, dp[cut])
             d = jnp.sum((e * dp[cut]).reshape(steps, 8, lanes), axis=0)
             e = jnp.sum(e.reshape(steps, 8, lanes), axis=0)
             acc_l = e if acc_l is None else acc_l + e
@@ -139,98 +147,145 @@
         return top, jnp.sum(acc_l, axis=0, keepdims=True), jnp.sum(acc_d, axis=0, keepdims=True)
 
 
-def merged(parts):
-    if len(parts) == 1:
-        return parts[0]
-    top = functools.reduce(jnp.maximum, [p[0] for p in parts])
-    weights = [jnp.exp2(p[0] - top) for p in parts]
-    return top, sum(p[1] * w for p, w in zip(parts, weights)), sum(p[2] * w for p, w in zip(parts, weights))
-
-
-def rect_stats(sh, keys, queries):
+def rect_shapes(sizes, keys, queries, wrap):
+    heads, rows = sizes[0], sizes[2]
+    shapes = [wrap((heads * 8, len(queries) * rows), jnp.float32)]
+    if 0 in keys:
+        shapes += [wrap((heads, rows, len(queries) * rows), jnp.float32)] * 2
+    if 0 in queries:
+        shapes += [wrap((heads, len(keys) * rows, rows), jnp.float32)] * 2
+    return shapes
+
+
+def rect_refs(refs, keys, queries):
+    refs = list(refs)
+    stat = refs.pop(0)
+    cols = (refs.pop(0), refs.pop(0)) if 0 in keys else None
+    rest = (refs.pop(0), refs.pop(0)) if 0 in queries else None
+    return stat, cols, rest
+
+
+def run_rect(sh, keys, queries, refs):
+    stat, cols, mine = rect_refs(refs, keys, queries)
     ids = sh.key_ids(keys)
-    found = {}
-    pairs = [queries[i : i + 2] for i in range(0, len(queries), 2)]
-    for group in pairs:
+    own = keys.index(0) * sh.blocks if 0 in keys else None
+    for first in range(0, len(queries), 2):
+        group = queries[first : first + 2]
+        lanes = slice(first * sh.rows, (first + len(group)) * sh.rows)
         bias = sh.bias(ids, group)
+        scored = [sh.scores(h, keys, group) for h in range(sh.heads)]
         for h in range(sh.heads):
-            got = sh.stats(sh.scores(h, keys, group), bias[h])
-            for i, s in enumerate(group):
-                found[h, s] = tuple(x[:, i * sh.rows : (i + 1) * sh.rows] for x in got)
-    return found
-
-
-def stats_kernel(sizes, slots_in, before, rects, *refs):
-    heads = sizes[0]
+
+            def keep(kb, cut, e, dp):
+                if own is not None and own <= kb < own + sh.blocks:
+                    part = slice((kb - own) * sh.block_rows, (kb - own + 1) * sh.block_rows)
+                    cols[0][h, part, lanes] = e
+                    cols[1][h, part, lanes] = dp
+                if 0 in group:
+                    place = slice(group.index(0) * sh.rows, (group.index(0) + 1) * sh.rows)
+                    mine[0][h, cut] = e[:, place]
+                    mine[1][h, cut] = dp[:, place]
+
+            for i, x in enumerate(sh.stats(scored[h], bias[h], keep)):
+                stat[8 * h + i : 8 * h + i + 1, lanes] = x
+
+
+def stats_kernel(sizes, slots_in, rects, *refs):
     n = len(slots_in)
-    a_refs = dict(zip(slots_in, refs[:n]))
-    b_refs = dict(zip(slots_in, refs[n : 2 * n]))
+    sh = Shards(sizes, dict(zip(slots_in, refs[:n])), dict(zip(slots_in, refs[n : 2 * n])))
     rest = refs[2 * n :]
-    old = rest[0] if before else None
-    out = rest[-1]
-    sh = Shards(sizes, a_refs, b_refs)
-    parts = {}
     for keys, queries in rects:
-        for where, got in rect_stats(sh, keys, queries).items():
-            parts.setdefault(where, []).append(got)
-    for (h, s), found in parts.items():
-        if s in before:
-            found.append(tuple(old[s, 3 * h + i : 3 * h + i + 1] for i in range(3)))
-        for i, x in enumerate(merged(found)):
-            out[s, 3 * h + i : 3 * h + i + 1] = x
-
-
-def final_kernel(sizes, before, rects, *refs):
-    heads, count = sizes[:2]
-    a_refs = dict(enumerate(refs[:count]))
-    b_refs = dict(enumerate(refs[count : 2 * count]))
-    old, dq_ref, dk_ref, dv_ref = refs[2 * count :]
-    sh = Shards(sizes, a_refs, b_refs)
-    every = list(range(count))
-    parts = {}
-    for keys, queries in rects:
-        for where, got in rect_stats(sh, keys, queries).items():
-            parts.setdefault(where, []).append(got)
+        size = len(rect_shapes(sizes, keys, queries, lambda *x: None))
+        run_rect(sh, keys, queries, rest[:size])
+        rest = rest[size:]
+
+
+def final_kernel(sizes, done, rects, *refs):
+    heads, count, rows = sizes[:3]
+    blocks = rows // sizes[4]
+    sh = Shards(sizes, dict(enumerate(refs[:count])), dict(enumerate(refs[count : 2 * count])))
+    rest = refs[2 * count :]
+    known = []
+    outputs = []
+    for group in (done, rects):
+        for keys, queries in group:
+            size = len(rect_shapes(sizes, keys, queries, lambda *x: None))
+            known.append((keys, queries, rect_refs(rest[:size], keys, queries)))
+            if group is rects:
+                run_rect(sh, keys, queries, rest[:size])
+            rest = rest[size:]
+        if group is done:
+            outputs, rest = rest[:3], rest[3:]
+    dq_ref, dk_ref, dv_ref = outputs
+    dq_buf, dk_buf, dv_buf, sems = rest
+
+    def part(found, h, i, s):
+        keys, queries, (stat, _, _) = found
+        lanes = slice(queries.index(s) * rows, (queries.index(s) + 1) * rows)
+        return stat[8 * h + i : 8 * h + i + 1, lanes]
+
     shift, dot_row = {}, {}
-    for (h, s), found in parts.items():
-        if s in before:
-            found.append(tuple(old[s, 3 * h + i : 3 * h + i + 1] for i in range(3)))
-        top, total, weighted = merged(found)
-        shift[h, s] = top + jnp.log2(total)
-        dot_row[h, s] = weighted / total
-    own_ids, all_ids = sh.key_ids([0]), sh.key_ids(every)
-    row_bias = sh.bias(all_ids, [0])
     for h in range(heads):
-        dk = dv = None
-        for first in range(0, count, 2):
-            group = every[first : first + 2]
-            bias = sh.bias(own_ids, group)[h]
-            s, dp = sh.scores(h, [0], group)
-            bias = bias - jnp.concatenate([shift[h, i] for i in group], axis=1)
-            dots = jnp.concatenate([dot_row[h, i] for i in group], axis=1)
-            p_low, ds_low = weights(sh, s, dp, bias, dots)
-            v_term = jnp.dot(p_low, sh.g(h, group), preferred_element_type=jnp.float32)
-            k_term = jnp.dot(ds_low, sh.q(h, group), preferred_element_type=jnp.float32)
-            dv = v_term if dv is None else dv + v_term
-            dk = k_term if dk is None else dk + k_term
-        dk_ref[h] = (dk * sh.scale).astype(dk_ref.dtype)
-        dv_ref[h] = dv.astype(dv_ref.dtype)
-        s, dp = sh.scores(h, every, [0])
-        _, ds_low = weights(sh, s, dp, row_bias[h] - shift[h, 0], dot_row[h, 0])
+        for s in range(count):
+            holds = [k for k in known if s in k[1]]
+            top = functools.reduce(jnp.maximum, [part(k, h, 0, s) for k in holds])
+            scales = [jnp.exp2(part(k, h, 0, s) - top) for k in holds]
+            total = sum(part(k, h, 1, s) * w for k, w in zip(holds, scales))
+            shift[h, s] = top + jnp.log2(total)
+            dot_row[h, s] = sum(part(k, h, 2, s) * w for k, w in zip(holds, scales)) / total
+
+    def weight(found, h, s):
+        return jnp.exp2(part(found, h, 0, s) - shift[h, s])
+
+    copies = []
+
+    def send(h, i, src, dst):
+        copies.append(pltpu.make_async_copy(src.at[h], dst.at[h], sems.at[3 * h + i]))
+        copies[-1].start()
+
+    steps = range(0, rows, sizes[4])
+    for h in range(heads):
+        order, low = [], []
+        for k in known:
+            keys, queries, (_, _, mine) = k
+            if 0 not in queries:
+                continue
+            order += keys
+            w = weight(k, h, 0)
+            for r in range(0, len(keys) * rows, sizes[4]):
+                cut = slice(r, r + sizes[4])
+                low.append(((mine[0][h, cut] * w) * (mine[1][h, cut] - dot_row[h, 0])).astype(jnp.bfloat16))
         dq = lax.dot_general(
-            ds_low, sh.k(h, every), (((0,), (0,)), ((), ())), preferred_element_type=jnp.float32
+            jnp.concatenate(low), sh.k(h, order), (((0,), (0,)), ((), ())),
+            preferred_element_type=jnp.float32,
         )
-        dq_ref[h] = (dq * sh.scale).astype(dq_ref.dtype)
-
-
-def weights(sh, s, dp, bias, dots):
-    p_low, ds_low = [], []
-    for kb in range(bias.shape[0]):
-        cut = slice(kb * sh.block_rows, (kb + 1) * sh.block_rows)
-        p = jnp.exp2(s[cut] * sh.rate + bias[kb : kb + 1])
-        p_low.append(p.astype(jnp.bfloat16))
-        ds_low.append((p * (dp[cut] - dots)).astype(jnp.bfloat16))
-    return jnp.concatenate(p_low), jnp.concatenate(ds_low)
+        dq_buf[h] = (dq * sh.scale).astype(dq_buf.dtype)
+        send(h, 0, dq_buf, dq_ref)
+    for h in range(heads):
+        order, p_low, ds_low = [], [], []
+        for k in known:
+            keys, queries, (_, cols, _) = k
+            if 0 not in keys:
+                continue
+            for s in queries:
+                order.append(s)
+                lanes = slice(queries.index(s) * rows, (queries.index(s) + 1) * rows)
+                w, dots = weight(k, h, s), dot_row[h, s]
+                p_col, ds_col = [], []
+                for r in steps:
+                    p = cols[0][h, r : r + sizes[4], lanes] * w
+                    p_col.append(p.astype(jnp.bfloat16))
+                    ds_col.append((p * (cols[1][h, r : r + sizes[4], lanes] - dots)).astype(jnp.bfloat16))
+                p_low.append(jnp.concatenate(p_col))
+                ds_low.append(jnp.concatenate(ds_col))
+        dv = jnp.dot(jnp.concatenate(p_low, axis=1), sh.g(h, order), preferred_element_type=jnp.float32)
+        dv_buf[h] = dv.astype(dv_buf.dtype)
+        send(h, 2, dv_buf, dv_ref)
+        dk = jnp.dot(jnp.concatenate(ds_low, axis=1), sh.q(h, order), preferred_element_type=jnp.float32)
+        dk_buf[h] = (dk * sh.scale).astype(dk_buf.dtype)
+        send(h, 1, dk_buf, dk_ref)
+    for c in copies:
+        c.wait()
 
 
 def near(arrays):
@@ -248,7 +303,6 @@
     sizes = (heads, count, rows, width, rows // blocks, slots, global_ids.shape[0])
     head_rows = -(-(heads * slots + 1 + global_ids.shape[0]) // 16) * 16
     vmem = pl.BlockSpec(memory_space=pltpu.VMEM)
-    smem = pl.BlockSpec(memory_space=pltpu.SMEM)
     anyspace = pl.BlockSpec(memory_space=pl.ANY)
     a, b = pl.pallas_call(
         functools.partial(pack_kernel, sizes),
@@ -256,16 +310,19 @@
             pltpu.VMEM((2 * heads * rows + head_rows, width), queries.dtype),
             pltpu.VMEM((2 * heads * rows, width), queries.dtype),
         ),
-        in_specs=[smem, smem] + [anyspace] * 4,
+        in_specs=[anyspace] * 6,
         out_specs=(vmem, vmem),
-        scratch_shapes=[pltpu.SemaphoreType.DMA((4 * heads,))],
+        scratch_shapes=[
+            pltpu.SMEM(rand_ids.shape, jnp.int32),
+            pltpu.SMEM(global_ids.shape, jnp.int32),
+            pltpu.SemaphoreType.DMA((2 + 4 * heads,)),
+        ],
     )(rand_ids, global_ids, keys, values, queries, grad_out)
 
     a_all, b_all = [a], [b]
     af = ab = a
     bf = bb = b
-    stat = None
-    stat_shape = pltpu.VMEM((count, 8, rows), jnp.float32)
+    done, left = [], []
     for d in range(1, half):
         af, ab = lax.ppermute(af, "seq", forward), lax.ppermute(ab, "seq", backward)
         bf, bb = lax.ppermute(bf, "seq", forward), lax.ppermute(bb, "seq", backward)
@@ -274,30 +331,33 @@
         if d < half - 2:
             continue
         now = list(range(2 * d + 1))
-        if stat is None:
-            before, rects = [], [(now, now)]
-        else:
-            before, new = now[:-2], now[-2:]
-            rects = [(new, before), (now, new)]
-        stat = pl.pallas_call(
-            functools.partial(stats_kernel, sizes, now, before, rects),
-            out_shape=stat_shape,
-            in_specs=[vmem] * (2 * len(now) + bool(before)),
-            out_specs=vmem,
+        rects = [(now[-2:], now[:-2]), (now, now[-2:])] if done else [(now, now)]
+        shapes = [x for r in rects for x in rect_shapes(sizes, *r, pltpu.VMEM)]
+        got = pl.pallas_call(
+            functools.partial(stats_kernel, sizes, now, rects),
+            out_shape=tuple(shapes),
+            compiler_params=pltpu.CompilerParams(vmem_limit_bytes=KERNEL_VMEM),
+            in_specs=[vmem] * (2 * len(now)),
+            out_specs=(vmem,) * len(shapes),
             cost_estimate=pl.CostEstimate(flops=10**9, bytes_accessed=10**6, transcendentals=10**6),
-        )(*near(a_all), *near(b_all), *near([stat] if before else []))
+        )(*near(a_all), *near(b_all))
+        done += rects
+        left += got
     a_all.append(lax.ppermute(af, "seq", forward))
     b_all.append(lax.ppermute(bb, "seq", backward))
     every = list(range(count))
-    before = every[:-1]
-    rects = [(every[-1:], before), (every, every[-1:])]
+    rects = [(every[-1:], every[:-1]), (every, every[-1:])]
     out = jax.ShapeDtypeStruct(queries.shape, queries.dtype)
+    buf = pltpu.VMEM(queries.shape, queries.dtype)
     return pl.pallas_call(
-        functools.partial(final_kernel, sizes, before, rects),
+        functools.partial(final_kernel, sizes, done, rects),
         out_shape=(out, out, out),
-        in_specs=[vmem] * (2 * count + 1),
-        out_specs=(vmem, vmem, vmem),
-    )(*near(a_all), *near(b_all), *near([stat]))
+        compiler_params=pltpu.CompilerParams(vmem_limit_bytes=KERNEL_VMEM),
+        in_specs=[vmem] * (2 * count + len(left)),
+        out_specs=(anyspace,) * 3,
+        scratch_shapes=[x for r in rects for x in rect_shapes(sizes, *r, pltpu.VMEM)]
+        + [buf, buf, buf, pltpu.SemaphoreType.DMA((3 * heads,))],
+    )(*near(a_all), *near(b_all), *near(left))
 
 
 def with_halo(value, sides, width):

time: 32.9 us -> 31.1 us (0.945)
  Pallas kernels: 8.31 us -> 6.56 us
    pallas_call x3, Pallas kernels: 6.67 us -> 5.6 us  [the longest x2 3.07 us: gathered(): pl.pallas_call(functools.partial(stats_kernel, sizes, now, rects), out_sh...]
    pallas_call x1, Pallas kernels: 1.64 us -> 0.96 us  [gathered(): pl.pallas_call(functools.partial(pack_kernel, sizes), out_shape=(pltpu.VM...]
  transfers between devices with their start and end apart: 14 -> 14, of which waited for: 4 -> 4; matrix products, arithmetic and copies ran while one was open for 0% -> 0% of each run, Pallas kernels for 9% -> 10%
where the time goes in v3:
time: 31.1 us; the launch traced here: 30.9 us
  starting transfers between devices  15.7 us (50%)
  waiting for transfers between devices  7.93 us (25%)
  Pallas kernels  6.56 us (21%)
  between operations  0.69 us (2%)
    ppermute x3, starting transfers between devices, gathered(): lax.ppermute(af, 'seq', forward)  7.16 us
    ppermute x3, waiting for transfers between devices, gathered(): lax.ppermute(ab, 'seq', backward)  5.02 us
    ppermute x3, starting transfers between devices, gathered(): lax.ppermute(bf, 'seq', forward)  3.99 us
    pallas_call x2, Pallas kernels, gathered(): pl.pallas_call(functools.partial(stats_kernel, sizes, now, rects), out_sh...  3.07 us
    pallas_call x1, Pallas kernels, gathered(): pl.pallas_call(functools.partial(final_kernel, sizes, done, rects), out_s...  2.53 us
    ppermute x3, starting transfers between devices, gathered(): lax.ppermute(ab, 'seq', backward)  2.1 us
    ppermute x1, starting transfers between devices, gathered(): a_all.append(lax.ppermute(af, 'seq', forward))  1.95 us
    ppermute x3, waiting for transfers between devices, gathered(): lax.ppermute(af, 'seq', forward)  1.93 us
  transfers between devices with their start and end apart: 14, of which 4 were waited for; matrix products, arithmetic and copies ran while one was open for 0% of the time, Pallas kernels for 10%

profile of v3, /device:TPU:0, one launch (start us, length us, event | category | flops | bytes accessed | tf_op | source)
XLA Modules:
  0.0 30.9 jit_solution(1918472875909078206)
XLA Ops:
  0.6 1.0 %shard_map.85 = (bf16[528,128]{1,0:T(8,128)(2,1)S(1)}, bf16[512,128]{1,0:T(8,128)(2,1)S(1)}) custom-call(s32[2,2,3]{2,1,0:T(2,128)} %ids_hbm.1, s32[2]{0:T(128)} %gids_hbm.1, bf16[2,128,128]{2,1,0:T(8,128)(2,1)} %k_ref.1, bf16[2,128,128]{2,1,0:T(8,128)(2,1)} %v_ref.1, bf16[2,128,128]{2,1,0:T(8,128)(2,1)} %q_ref.1, bf16[2,128,128]{2,1,0:T(8,128)(2,1)} %g_ref.1), custom_call_target="tpu_custom_call" | custom-call | tf_op jit(solution)/shard_map/pallas_call | solution.py:307
  1.6 3.1 %collective-permute-start = (bf16[528,128]{1,0:T(8,128)(2,1)S(1)}, bf16[528,128]{1,0:T(8,128)(2,1)S(1)}, u32[]{:S(2)}, u32[]{:S(2)}) collective-permute-start(bf16[528,128]{1,0:T(8,128)(2,1)S(1)} %get-tuple-element.16.refs_0_), channel_id=1, source_target_pairs={{0,8},{8,16},{16,24},{24,28},{28,20},{20,12},{12,4},{4,0},{1,9},{9... | collective-permute-start | bytes 405512 | tf_op jit(solution)/shard_map/ppermute | solution.py:327
  4.7 0.0 collective-permute-start.8
  4.7 2.0 %collective-permute-start.1 = (bf16[528,128]{1,0:T(8,128)(2,1)S(1)}, bf16[528,128]{1,0:T(8,128)(2,1)S(1)}, u32[]{:S(2)}, u32[]{:S(2)}) collective-permute-start(bf16[528,128]{1,0:T(8,128)(2,1)S(1)} %get-tuple-element.16.refs_0_), channel_id=1, source_target_pairs={{8,0},{16,8},{24,16},{28,24},{20,28},{12,20},{4,12},{0,4},{9,1},{1... | collective-permute-start | bytes 405512 | tf_op jit(solution)/shard_map/ppermute | solution.py:327
  6.7 0.1 collective-permute-start.7
  6.8 1.9 %collective-permute-done.refs_1_ = bf16[528,128]{1,0:T(8,128)(2,1)S(1)} collective-permute-done((bf16[528,128]{1,0:T(8,128)(2,1)S(1)}, bf16[528,128]{1,0:T(8,128)(2,1)S(1)}, u32[]{:S(2)}, u32[]{:S(2)}) %collective-permute-start) | collective-permute-done | bytes 135200 | tf_op jit(solution)/shard_map/ppermute | solution.py:327
  8.7 2.5 %collective-permute-start.2 = (bf16[528,128]{1,0:T(8,128)(2,1)S(1)}, bf16[528,128]{1,0:T(8,128)(2,1)S(1)}, u32[]{:S(2)}, u32[]{:S(2)}) collective-permute-start(bf16[528,128]{1,0:T(8,128)(2,1)S(1)} %collective-permute-done.refs_1_), channel_id=1, source_target_pairs={{0,8},{8,16},{16,24},{24,28},{28,20},{20,12},{12,4},{4,0},{1,9},{9... | collective-permute-start | bytes 405512 | tf_op jit(solution)/shard_map/ppermute | solution.py:327
  11.2 0.0 collective-permute-done.8.refs_7_.refs_9_.refs_10_
  11.2 0.0 collective-permute-start.10
  11.2 2.6 %collective-permute-done.1.refs_2_ = bf16[528,128]{1,0:T(8,128)(2,1)S(1)} collective-permute-done((bf16[528,128]{1,0:T(8,128)(2,1)S(1)}, bf16[528,128]{1,0:T(8,128)(2,1)S(1)}, u32[]{:S(2)}, u32[]{:S(2)}) %collective-permute-start.1) | collective-permute-done | bytes 135200 | tf_op jit(solution)/shard_map/ppermute | solution.py:327
  13.8 0.1 collective-permute-start.3
  13.9 0.0 collective-permute-done.7.refs_6_.refs_8_.refs_9_
  13.9 2.0 %collective-permute-start.9 = (bf16[512,128]{1,0:T(8,128)(2,1)S(1)}, bf16[512,128]{1,0:T(8,128)(2,1)S(1)}, u32[]{:S(2)}, u32[]{:S(2)}) collective-permute-start(bf16[512,128]{1,0:T(8,128)(2,1)S(1)} %collective-permute-done.7.refs_6_.refs_8_.refs_9_), channel_id=1, source_target_pairs={{0,8},{8,16},{16,24},{24,28},{28,20},{20,12},{12,4},{4,0},{1,9},{9... | collective-permute-start | bytes 393224 | tf_op jit(solution)/shard_map/ppermute | solution.py:328
  15.8 0.0 collective-permute-done.2.refs_3_
  15.8 1.6 %collective-permute-start.4 = (bf16[528,128]{1,0:T(8,128)(2,1)S(1)}, bf16[528,128]{1,0:T(8,128)(2,1)S(1)}, u32[]{:S(2)}, u32[]{:S(2)}) collective-permute-start(bf16[528,128]{1,0:T(8,128)(2,1)S(1)} %collective-permute-done.2.refs_3_), channel_id=1, source_target_pairs={{0,8},{8,16},{16,24},{24,28},{28,20},{20,12},{12,4},{4,0},{1,9},{9... | collective-permute-start | bytes 405512 | tf_op jit(solution)/shard_map/ppermute | solution.py:327
  17.4 0.0 collective-permute-done.10.refs_9_.refs_11_.refs_12_
  17.4 0.4 %collective-permute-start.12 = (bf16[512,128]{1,0:T(8,128)(2,1)S(1)}, bf16[512,128]{1,0:T(8,128)(2,1)S(1)}, u32[]{:S(2)}, u32[]{:S(2)}) collective-permute-start(bf16[512,128]{1,0:T(8,128)(2,1)S(1)} %collective-permute-done.10.refs_9_.refs_11_.refs_12_), channel_id=1, source_target_pairs={{8,0},{16,8},{24,16},{28,24},{20,28},{12,20},{4,12},{0,4},{9,1},{1... | collective-permute-start | bytes 393224 | tf_op jit(solution)/shard_map/ppermute | solution.py:328
  17.9 2.4 %collective-permute-done.3.refs_4_ = bf16[528,128]{1,0:T(8,128)(2,1)S(1)} collective-permute-done((bf16[528,128]{1,0:T(8,128)(2,1)S(1)}, bf16[528,128]{1,0:T(8,128)(2,1)S(1)}, u32[]{:S(2)}, u32[]{:S(2)}) %collective-permute-start.3) | collective-permute-done | bytes 135200 | tf_op jit(solution)/shard_map/ppermute | solution.py:327
  20.2 0.1 collective-permute-start.5
  20.3 0.0 collective-permute-done.9.refs_8_.refs_10_.refs_11_
  20.3 2.0 %collective-permute-start.11 = (bf16[512,128]{1,0:T(8,128)(2,1)S(1)}, bf16[512,128]{1,0:T(8,128)(2,1)S(1)}, u32[]{:S(2)}, u32[]{:S(2)}) collective-permute-start(bf16[512,128]{1,0:T(8,128)(2,1)S(1)} %collective-permute-done.9.refs_8_.refs_10_.refs_11_), channel_id=1, source_target_pairs={{0,8},{8,16},{16,24},{24,28},{28,20},{20,12},{12,4},{4,0},{1,9},{9... | collective-permute-start | bytes 393224 | tf_op jit(solution)/shard_map/ppermute | solution.py:328
  22.3 1.0 %collective-permute-done.12.refs_13_.refs_14_ = bf16[512,128]{1,0:T(8,128)(2,1)S(1)} collective-permute-done((bf16[512,128]{1,0:T(8,128)(2,1)S(1)}, bf16[512,128]{1,0:T(8,128)(2,1)S(1)}, u32[]{:S(2)}, u32[]{:S(2)}) %collective-permute-start.12) | collective-permute-done | bytes 131104 | tf_op jit(solution)/shard_map/ppermute | solution.py:328
  23.2 0.1 collective-permute-start.13
  23.3 0.0 collective-permute-done.4.refs_5_
  23.3 2.0 %collective-permute-start.6 = (bf16[528,128]{1,0:T(8,128)(2,1)S(1)}, bf16[528,128]{1,0:T(8,128)(2,1)S(1)}, u32[]{:S(2)}, u32[]{:S(2)}) collective-permute-start(bf16[528,128]{1,0:T(8,128)(2,1)S(1)} %collective-permute-done.4.refs_5_), channel_id=1, source_target_pairs={{0,8},{8,16},{16,24},{24,28},{28,20},{20,12},{12,4},{4,0},{1,9},{9... | collective-permute-start | bytes 405512 | tf_op jit(solution)/shard_map/ppermute | solution.py:346
  25.3 1.6 %shard_map.86 = (f32[16,640]{1,0:T(8,128)S(1)}, f32[2,128,640]{2,1,0:T(8,128)S(1)}, f32[2,128,640]{2,1,0:T(8,128)S(1)}, f32[2,640,128]{2,1,0:T(8,128)S(1)}, f32[2,640,128]{2,1,0:T(8,128)S(1)}) custom-call(bf16[528,128]{1,0:T(8,128)(2,1)S(1)} %get-tuple-element.16.refs_0_, bf16[528,128]{1,0:T(8,128)(2,1)S(1)} %collective-permute-done.refs_1_, ...), custom_call_target="tpu_custom_call" | custom-call | flops 1000000000 | bytes 1000000 | tf_op jit(solution)/shard_map/pallas_call | solution.py:336
  26.9 0.0 collective-permute-done.11.refs_12_.refs_13_
  26.9 0.0 collective-permute-done.5.refs_6_
  26.9 1.5 %shard_map.87 = (f32[16,640]{1,0:T(8,128)S(1)}, f32[2,256,128]{2,1,0:T(8,128)S(1)}, f32[2,256,128]{2,1,0:T(8,128)S(1)}, f32[16,256]{1,0:T(8,128)S(1)}, f32[2,128...) custom-call(bf16[528,128]{1,0:T(8,128)(2,1)S(1)} %get-tuple-element.16.refs_0_, ...), custom_call_target="tpu_custom_call" | custom-call | flops 1000000000 | bytes 1000000 | tf_op jit(solution)/shard_map/pallas_call | solution.py:336
  28.4 0.0 collective-permute-done.13.refs_15_
  28.4 0.0 collective-permute-done.6.refs_7_
  28.4 2.5 %shard_map.88 = (bf16[2,128,128]{2,1,0:T(8,128)(2,1)}, bf16[2,128,128]{2,1,0:T(8,128)(2,1)}, bf16[2,128,128]{2,1,0:T(8,128)(2,1)}) custom-call(bf16[528,128]{1,0:T(8,128)(2,1)S(1)} %get-tuple-element.16.refs_0_, bf16[528,128]{1,0:T(8,128)(2,1)S(1)} %collective-permute-done.refs_1_, bf16[528,128]{1,0:T(8,128)(2,1)S(1)} %collective-permute-done.1.refs_2_, ...), custom_call_target="tpu_custom_call" | custom-call | tf_op jit(solution)/shard_map/pallas_call | solution.py:352
Async XLA Ops:
  1.6 7.1 %collective-permute-start = (bf16[528,128]{1,0:T(8,128)(2,1)S(1)}, bf16[528,128]{1,0:T(8,128)(2,1)S(1)}, u32[]{:S(2)}, u32[]{:S(2)}) collective-permute-start(bf16[528,128]{1,0:T(8,128)(2,1)S(1)} %get-tuple-element.16.refs_0_), channel_id=1, source_target_pairs={{0,8},{8,16},{16,24},{24,28},{28,20},{20,12},{12,4},{4,0},{1,9},{9... | collective-permute-start | bytes 405512 | tf_op jit(solution)/shard_map/ppermute | solution.py:327
  4.7 6.5 %collective-permute-start.8 = (bf16[512,128]{1,0:T(8,128)(2,1)S(1)}, bf16[512,128]{1,0:T(8,128)(2,1)S(1)}, u32[]{:S(2)}, u32[]{:S(2)}) collective-permute-start(bf16[512,128]{1,0:T(8,128)(2,1)S(1)} %get-tuple-element.17.refs_5_.refs_7_.refs_8_), channel_id=1, source_target_pairs={{8,0},{16,8},{24,16},{28,24},{20,28},{12,20},{4,12},{0,4},{9,1},{1... | collective-permute-start | bytes 393224 | tf_op jit(solution)/shard_map/ppermute | solution.py:328
  4.7 9.1 %collective-permute-start.1 = (bf16[528,128]{1,0:T(8,128)(2,1)S(1)}, bf16[528,128]{1,0:T(8,128)(2,1)S(1)}, u32[]{:S(2)}, u32[]{:S(2)}) collective-permute-start(bf16[528,128]{1,0:T(8,128)(2,1)S(1)} %get-tuple-element.16.refs_0_), channel_id=1, source_target_pairs={{8,0},{16,8},{24,16},{28,24},{20,28},{12,20},{4,12},{0,4},{9,1},{1... | collective-permute-start | bytes 405512 | tf_op jit(solution)/shard_map/ppermute | solution.py:327
  6.7 7.2 %collective-permute-start.7 = (bf16[512,128]{1,0:T(8,128)(2,1)S(1)}, bf16[512,128]{1,0:T(8,128)(2,1)S(1)}, u32[]{:S(2)}, u32[]{:S(2)}) collective-permute-start(bf16[512,128]{1,0:T(8,128)(2,1)S(1)} %get-tuple-element.17.refs_5_.refs_7_.refs_8_), channel_id=1, source_target_pairs={{0,8},{8,16},{16,24},{24,28},{28,20},{20,12},{12,4},{4,0},{1,9},{9... | collective-permute-start | bytes 393224 | tf_op jit(solution)/shard_map/ppermute | solution.py:328
  8.7 7.1 %collective-permute-start.2 = (bf16[528,128]{1,0:T(8,128)(2,1)S(1)}, bf16[528,128]{1,0:T(8,128)(2,1)S(1)}, u32[]{:S(2)}, u32[]{:S(2)}) collective-permute-start(bf16[528,128]{1,0:T(8,128)(2,1)S(1)} %collective-permute-done.refs_1_), channel_id=1, source_target_pairs={{0,8},{8,16},{16,24},{24,28},{28,20},{20,12},{12,4},{4,0},{1,9},{9... | collective-permute-start | bytes 405512 | tf_op jit(solution)/shard_map/ppermute | solution.py:327
  11.2 6.2 %collective-permute-start.10 = (bf16[512,128]{1,0:T(8,128)(2,1)S(1)}, bf16[512,128]{1,0:T(8,128)(2,1)S(1)}, u32[]{:S(2)}, u32[]{:S(2)}) collective-permute-start(bf16[512,128]{1,0:T(8,128)(2,1)S(1)} %collective-permute-done.8.refs_7_.refs_9_.refs_10_), channel_id=1, source_target_pairs={{8,0},{16,8},{24,16},{28,24},{20,28},{12,20},{4,12},{0,4},{9,1},{1... | collective-permute-start | bytes 393224 | tf_op jit(solution)/shard_map/ppermute | solution.py:328
  13.8 6.5 %collective-permute-start.3 = (bf16[528,128]{1,0:T(8,128)(2,1)S(1)}, bf16[528,128]{1,0:T(8,128)(2,1)S(1)}, u32[]{:S(2)}, u32[]{:S(2)}) collective-permute-start(bf16[528,128]{1,0:T(8,128)(2,1)S(1)} %collective-permute-done.1.refs_2_), channel_id=1, source_target_pairs={{8,0},{16,8},{24,16},{28,24},{20,28},{12,20},{4,12},{0,4},{9,1},{1... | collective-permute-start | bytes 405512 | tf_op jit(solution)/shard_map/ppermute | solution.py:327
  13.9 6.5 %collective-permute-start.9 = (bf16[512,128]{1,0:T(8,128)(2,1)S(1)}, bf16[512,128]{1,0:T(8,128)(2,1)S(1)}, u32[]{:S(2)}, u32[]{:S(2)}) collective-permute-start(bf16[512,128]{1,0:T(8,128)(2,1)S(1)} %collective-permute-done.7.refs_6_.refs_8_.refs_9_), channel_id=1, source_target_pairs={{0,8},{8,16},{16,24},{24,28},{28,20},{20,12},{12,4},{4,0},{1,9},{9... | collective-permute-start | bytes 393224 | tf_op jit(solution)/shard_map/ppermute | solution.py:328
  15.8 7.5 %collective-permute-start.4 = (bf16[528,128]{1,0:T(8,128)(2,1)S(1)}, bf16[528,128]{1,0:T(8,128)(2,1)S(1)}, u32[]{:S(2)}, u32[]{:S(2)}) collective-permute-start(bf16[528,128]{1,0:T(8,128)(2,1)S(1)} %collective-permute-done.2.refs_3_), channel_id=1, source_target_pairs={{0,8},{8,16},{16,24},{24,28},{28,20},{20,12},{12,4},{4,0},{1,9},{9... | collective-permute-start | bytes 405512 | tf_op jit(solution)/shard_map/ppermute | solution.py:327
  17.4 5.8 %collective-permute-start.12 = (bf16[512,128]{1,0:T(8,128)(2,1)S(1)}, bf16[512,128]{1,0:T(8,128)(2,1)S(1)}, u32[]{:S(2)}, u32[]{:S(2)}) collective-permute-start(bf16[512,128]{1,0:T(8,128)(2,1)S(1)} %collective-permute-done.10.refs_9_.refs_11_.refs_12_), channel_id=1, source_target_pairs={{8,0},{16,8},{24,16},{28,24},{20,28},{12,20},{4,12},{0,4},{9,1},{1... | collective-permute-start | bytes 393224 | tf_op jit(solution)/shard_map/ppermute | solution.py:328
  20.2 6.6 %collective-permute-start.5 = (bf16[528,128]{1,0:T(8,128)(2,1)S(1)}, bf16[528,128]{1,0:T(8,128)(2,1)S(1)}, u32[]{:S(2)}, u32[]{:S(2)}) collective-permute-start(bf16[528,128]{1,0:T(8,128)(2,1)S(1)} %collective-permute-done.3.refs_4_), channel_id=1, source_target_pairs={{8,0},{16,8},{24,16},{28,24},{20,28},{12,20},{4,12},{0,4},{9,1},{1... | collective-permute-start | bytes 405512 | tf_op jit(solution)/shard_map/ppermute | solution.py:327
  20.3 6.5 %collective-permute-start.11 = (bf16[512,128]{1,0:T(8,128)(2,1)S(1)}, bf16[512,128]{1,0:T(8,128)(2,1)S(1)}, u32[]{:S(2)}, u32[]{:S(2)}) collective-permute-start(bf16[512,128]{1,0:T(8,128)(2,1)S(1)} %collective-permute-done.9.refs_8_.refs_10_.refs_11_), channel_id=1, source_target_pairs={{0,8},{8,16},{16,24},{24,28},{28,20},{20,12},{12,4},{4,0},{1,9},{9... | collective-permute-start | bytes 393224 | tf_op jit(solution)/shard_map/ppermute | solution.py:328
  23.2 5.1 %collective-permute-start.13 = (bf16[512,128]{1,0:T(8,128)(2,1)S(1)}, bf16[512,128]{1,0:T(8,128)(2,1)S(1)}, u32[]{:S(2)}, u32[]{:S(2)}) collective-permute-start(bf16[512,128]{1,0:T(8,128)(2,1)S(1)} %collective-permute-done.12.refs_13_.refs_14_), channel_id=1, source_target_pairs={{8,0},{16,8},{24,16},{28,24},{20,28},{12,20},{4,12},{0,4},{9,1},{1... | collective-permute-start | bytes 393224 | tf_op jit(solution)/shard_map/ppermute | solution.py:347
  23.3 5.1 %collective-permute-start.6 = (bf16[528,128]{1,0:T(8,128)(2,1)S(1)}, bf16[528,128]{1,0:T(8,128)(2,1)S(1)}, u32[]{:S(2)}, u32[]{:S(2)}) collective-permute-start(bf16[528,128]{1,0:T(8,128)(2,1)S(1)} %collective-permute-done.4.refs_5_), channel_id=1, source_target_pairs={{0,8},{8,16},{16,24},{24,28},{28,20},{20,12},{12,4},{4,0},{1,9},{9... | collective-permute-start | bytes 405512 | tf_op jit(solution)/shard_map/ppermute | solution.py:346
